TPU v7x, 512 devices: a whole 4x8x8 slice. The times are simulated.
512 devices in a mesh: rows: 16 (over x, y_lo, core), dp: 32 (over z, y_hi).
Axes of the slice: x: 4, y: 8 (y_hi: 4, y_lo: 2; y = y_hi * 2 + y_lo), z: 8, core: 2. Of those that a mesh axis runs over, the one named last changes fastest.
Arguments:
- images: bfloat16 [32, 32, 512, 128], P('dp', 'rows'), may hold values from -54 to 54
- conv_weight: bfloat16 [3, 3, 128, 128], replicated, may hold values from -0.1875 to 0.1875
- conv_bias: float32 [128], replicated, may hold values from -3 to 3
- norm_gain: float32 [128], replicated, may hold values from 0.5 to 1.5
- norm_shift: float32 [128], replicated, may hold values from -3 to 3
- down_weight: bfloat16 [3, 3, 128, 256], replicated, may hold values from -0.1875 to 0.1875
- down_bias: float32 [256], replicated, may hold values from -3 to 3
- cotangent: bfloat16 [32, 16, 256, 256], P('dp', 'rows'), may hold values from -6 to 6
Outputs:
- block_out: bfloat16 [32, 16, 256, 256], P('dp', 'rows')
- grad_images: bfloat16 [32, 32, 512, 128], P('dp', 'rows')
- grad_conv_weight: float32 [3, 3, 128, 128], P(None, None, None, 'dp')
- grad_conv_bias: float32 [128], P('dp')
- grad_gain: float32 [128], P('dp')
- grad_shift: float32 [128], P('dp')
- grad_down_weight: float32 [3, 3, 128, 256], P(None, None, None, 'dp')
- grad_down_bias: float32 [256], P('dp')
All inputs are finite; a program needn't handle non-finite values.
Results may differ from a plain program's by a relative error of at most 0.0048.
Values may be sent and summed in bfloat16 or wider, within the bound.
A program may use at most 64 MiB of HBM per device.

v0:
```python
import jax
import jax.numpy as jnp
from jax import lax
from jax.sharding import PartitionSpec as P

GROUPS = 32


def extended(block, sides, width):
    for axis, dim in sides:
        count = lax.axis_size(axis)
        forward = [(i, i + 1) for i in range(count - 1)]
        backward = [(target, source) for source, target in forward]
        low = lax.ppermute(
            lax.slice_in_dim(block, block.shape[dim] - width, None, axis=dim), axis, forward
        )
        high = lax.ppermute(lax.slice_in_dim(block, 0, width, axis=dim), axis, backward)
        block = jnp.concatenate([low, block, high], axis=dim)
    return block


def from_behind(x, axis, by):
    length = lax.axis_size(axis)
    pairs = [(i, i + by) for i in range(length) if 0 <= i + by < length]
    return lax.ppermute(x, axis, pairs)


def taps_conv(padded, weight, rows, cols):
    total = jnp.zeros((rows * cols, weight.shape[3]), jnp.float32)
    for kh in range(3):
        for kw in range(3):
            piece = padded[kh : kh + rows, kw : kw + cols].reshape(rows * cols, -1)
            total = total + jnp.dot(piece, weight[kh, kw], preferred_element_type=jnp.float32)
    return total.reshape(rows, cols, weight.shape[3])


def weave(part_zero, part_one, part_two, axis):
    lead = [(0, 0)] * part_zero.ndim
    after = list(lead)
    before = list(lead)
    after[axis] = (0, 1)
    before[axis] = (1, 0)
    even = jnp.pad(part_zero, after) + jnp.pad(part_two, before)
    odd = jnp.pad(part_one, after)
    joined = jnp.stack([even, odd], axis + 1)
    shape = list(even.shape)
    shape[axis] = 2 * shape[axis]
    return joined.reshape(shape)


def shards(
    images, conv_weight, conv_bias, norm_gain, norm_shift, down_weight, down_bias, cotangent
):
    image = images[0]
    cot = cotangent[0]
    rows, cols, chans = image.shape
    half_rows, half_cols, outs = cot.shape
    width = chans // GROUPS
    count = float(rows * cols * width * lax.axis_size("rows"))
    framed = extended(image, (("rows", 0),), 1)
    padded = jnp.pad(framed, ((0, 0), (1, 1), (0, 0)))
    hidden = taps_conv(padded, conv_weight, rows, cols) + conv_bias
    grouped = hidden.reshape(rows, cols, GROUPS, width)
    mean = lax.psum(jnp.sum(grouped, axis=(0, 1, 3)), "rows") / count
    centred = grouped - mean[:, None]
    var = lax.psum(jnp.sum(centred * centred, axis=(0, 1, 3)), "rows") / count
    rstd = lax.rsqrt(var + 1e-05)
    normed = (centred * rstd[:, None]).reshape(rows, cols, chans)
    pre = normed * norm_gain + norm_shift
    sig = jax.nn.sigmoid(pre)
    mixed = (image.astype(jnp.float32) + pre * sig).astype(jnp.bfloat16)
    above = from_behind(mixed[-1], "rows", 1)
    shifted = jnp.pad(jnp.concatenate([above[None], mixed], 0), ((0, 0), (1, 0), (0, 0)))
    cot_flat = cot.reshape(half_rows * half_cols, outs)
    out = jnp.zeros((half_rows * half_cols, outs), jnp.float32)
    grad_down = []
    backs = []
    for kh in range(3):
        line = []
        back_line = []
        for kw in range(3):
            piece = shifted[kh : kh + 2 * half_rows : 2, kw : kw + 2 * half_cols : 2].reshape(
                half_rows * half_cols, chans
            )
            out = out + jnp.dot(piece, down_weight[kh, kw], preferred_element_type=jnp.float32)
            line.append(jnp.dot(piece.T, cot_flat, preferred_element_type=jnp.float32))
            back = jnp.dot(cot_flat, down_weight[kh, kw].T, preferred_element_type=jnp.float32)
            back_line.append(back.reshape(half_rows, half_cols, chans))
        grad_down.append(jnp.stack(line))
        backs.append(weave(back_line[0], back_line[1], back_line[2], 1))
    block = (out + down_bias).astype(jnp.bfloat16).reshape(half_rows, half_cols, outs)
    grad_down = jnp.stack(grad_down)
    grad_down_bias = jnp.sum(cot.astype(jnp.float32), axis=(0, 1))
    woven = weave(backs[0], backs[1], backs[2], 0)
    local_grad = woven[1 : rows + 1, 1 : cols + 1]
    from_below = from_behind(woven[0, 1 : cols + 1], "rows", -1)
    grad_mixed = jnp.concatenate([local_grad[:-1], local_grad[-1:] + from_below[None]], 0)
    grad_pre = grad_mixed * sig * (1.0 + pre * (1.0 - sig))
    grad_gain = jnp.sum(grad_pre * normed, axis=(0, 1))
    grad_shift = jnp.sum(grad_pre, axis=(0, 1))
    scaled = (grad_pre * norm_gain).reshape(rows, cols, GROUPS, width)
    normed_g = normed.reshape(rows, cols, GROUPS, width)
    first, second = lax.psum(
        (jnp.sum(scaled, axis=(0, 1, 3)), jnp.sum(scaled * normed_g, axis=(0, 1, 3))), "rows"
    )
    first = first / count
    second = second / count
    grad_hidden = (rstd[:, None] * (scaled - first[:, None] - normed_g * second[:, None])).reshape(
        rows, cols, chans
    )
    grad_bias = jnp.sum(grad_hidden, axis=(0, 1))
    rounded = grad_hidden.astype(jnp.bfloat16)
    flat = rounded.reshape(rows * cols, chans)
    grad_conv = []
    for kh in range(3):
        line = []
        for kw in range(3):
            piece = padded[kh : kh + rows, kw : kw + cols].reshape(rows * cols, chans)
            line.append(jnp.dot(piece.T, flat, preferred_element_type=jnp.float32))
        grad_conv.append(jnp.stack(line))
    grad_conv = jnp.stack(grad_conv)
    grad_framed = extended(rounded, (("rows", 0),), 1)
    grad_pad = jnp.pad(grad_framed, ((0, 0), (1, 1), (0, 0)))
    back_total = jnp.zeros((rows * cols, chans), jnp.float32)
    for kh in range(3):
        for kw in range(3):
            piece = grad_pad[2 - kh : 2 - kh + rows, 2 - kw : 2 - kw + cols].reshape(
                rows * cols, chans
            )
            back_total = back_total + jnp.dot(
                piece, conv_weight[kh, kw].T, preferred_element_type=jnp.float32
            )
    grad_image = (grad_mixed + back_total.reshape(rows, cols, chans)).astype(jnp.bfloat16)
    conv_pack = grad_conv.reshape(9 * chans, chans)
    small_pack = jnp.stack([grad_bias, grad_gain, grad_shift])
    down_pack = grad_down.reshape(9 * chans, outs)
    bias_pack = grad_down_bias[None]
    count_dp = lax.axis_size("dp")
    totals = lax.psum((conv_pack, small_pack, down_pack, bias_pack), ("rows", "dp"))
    owner = lax.axis_index("dp")
    narrow = chans // count_dp
    wide = outs // count_dp
    conv_part = lax.dynamic_slice_in_dim(totals[0], owner * narrow, narrow, 1)
    small_part = lax.dynamic_slice_in_dim(totals[1], owner * narrow, narrow, 1)
    down_part = lax.dynamic_slice_in_dim(totals[2], owner * wide, wide, 1)
    bias_part = lax.dynamic_slice_in_dim(totals[3], owner * wide, wide, 1)
    return (
        block[None],
        grad_image[None],
        conv_part.reshape(3, 3, chans, -1),
        small_part[0],
        small_part[1],
        small_part[2],
        down_part.reshape(3, 3, chans, -1),
        bias_part[0],
    )


def solution(mesh):
    in_specs = (
        P("dp", "rows", None, None),
        P(),
        P(),
        P(),
        P(),
        P(),
        P(),
        P("dp", "rows", None, None),
    )
    out_specs = (
        P("dp", "rows", None, None),
        P("dp", "rows", None, None),
        P(None, None, None, "dp"),
        P("dp"),
        P("dp"),
        P("dp"),
        P(None, None, None, "dp"),
        P("dp"),
    )
    return jax.shard_map(shards, mesh=mesh, in_specs=in_specs, out_specs=out_specs, check_vma=False)
```

profile of v0, /device:TPU:1, one launch (start us, length us, event | category | flops | bytes accessed | tf_op | source)
XLA Modules:
  0.0 581.2 jit_solution(11627743747505670904)
XLA Ops:
  7.2 1.1 copy.33
  8.4 0.7 slice_bitcast_fusion.3
  9.1 4.6 collective-permute-start
  13.7 5.5 collective-permute-start.1
  19.2 1.1 convolution_bitcast_fusion.17
  24.5 1.0 slice_bitcast_fusion.7
  25.5 1.9 collective-permute-start.3
  27.5 1.0 concatenate.65
  29.1 1.0 pad_maximum_fusion.10
  30.0 0.8 copy.42
  30.9 0.8 copy.37
  31.7 1.3 select_maximum_fusion.2
  33.0 1.1 fusion.142
  34.1 1.8 copy.43
  35.9 1.8 copy.41
  37.7 0.8 copy.40
  38.5 0.8 copy.39
  39.3 0.8 copy.38
  40.4 1.0 fusion.108
  41.4 1.2 convolution_add_fusion.15
  46.1 25.3 %psum.56 = f32[32]{0:T(128)S(1)} all-reduce(f32[32]{0:T(128)S(1)} %reduce_sum.83), channel_id=1, replica_groups=mesh['rows'=16,'dp'=32] {'rows'}, use_global_device_ids=true, to_apply=%region_2.3 | all-reduce | flops 32 | bytes 256 | tf_op jit(solution)/shard_map/psum | solution.py:64
  71.9 30.0 %psum.57 = f32[32]{0:T(128)S(1)} all-reduce(f32[32]{0:T(128)S(1)} %reduce_sum.105), channel_id=1, replica_groups=mesh['rows'=16,'dp'=32] {'rows'}, use_global_device_ids=true, to_apply=%region_5.6 | all-reduce | flops 32 | bytes 256 | tf_op jit(solution)/shard_map/psum | solution.py:66
  102.0 1.0 copy.44
  103.0 1.1 slice_add_fusion
  106.4 27.1 %all-reduce.17 = (f32[32]{0:T(128)S(1)}, f32[32]{0:T(128)S(1)}) all-reduce(f32[32]{0:T(128)S(1)} %reduce_sum.111, f32[32]{0:T(128)S(1)} %reduce_sum.108), channel_id=1, replica_groups=mesh['rows'=16,'dp'=32] {'rows'}, use_global_device_ids=true, to_apply=%region_11.12 | all-reduce | flops 64 | bytes 512 | tf_op jit(solution)/shard_map/psum | solution.py:103
  134.9 1.8 multiply_convert_fusion
  136.8 0.8 convolution_bitcast_fusion.22
  137.6 0.9 convolution_bitcast_fusion.23
  138.5 0.9 convolution_bitcast_fusion.24
  139.4 0.9 convolution_bitcast_fusion.25
  140.3 0.8 convolution_bitcast_fusion.26
  141.1 0.9 convolution_bitcast_fusion.21
  142.0 0.7 fusion.143
  143.0 1.1 fusion.128
  144.4 101.7 %all-reduce.15 = (f32[3,128]{1,0:T(4,128)S(1)}, f32[1,256]{1,0:T(1,128)S(1)}) all-reduce(f32[3,128]{1,0:T(4,128)S(1)} %pad_maximum_fusion.12, f32[1,256]{1,0:T(1,128)S(1)} %bitcast.406), channel_id=1, replica_groups=mesh['rows'=16,'dp'=32] {'rows','dp'}, use_global_device_ids=true, to_apply=%region_16.17 | all-reduce | flops 640 | bytes 5120 | tf_op jit(solution)/shard_map/psum | solution.py:139
  246.9 0.7 slice_bitcast_fusion.1
  247.6 4.4 collective-permute-start.2
  252.0 1.1 convolution_bitcast_fusion.18
  253.5 1.1 copy.70
  254.6 2.0 collective-permute-start.4
  256.6 3.0 collective-permute-start.5
  260.3 1.1 fusion.9
  261.4 2.4 slice.255
  263.8 2.4 slice.253
  266.2 2.4 slice.251
  268.5 2.4 slice.249
  270.9 2.4 slice.247
  273.3 2.4 slice.245
  275.6 2.4 slice.243
  278.0 2.4 slice.241
  280.4 2.6 slice.257
  284.9 1.4 copy.71
  287.0 1.0 pad_maximum_fusion.8
  288.2 0.8 copy.53
  289.1 1.3 select_maximum_fusion
  290.8 0.8 copy.60
  291.6 0.8 copy.58
  292.7 0.8 copy.55
  297.7 0.7 copy-done.11
  298.7 0.8 copy.72
  300.2 0.9 fusion.3
  301.1 270.4 %all-reduce.20.cloned.1.call-done = (f32[1152,128]{0,1:T(8,128)}, f32[1152,256]{0,1:T(8,128)}) async-done(((f32[1152,128]{0,1:T(8,128)}, f32[1152,256]{0,1:T(8,128)}), (f32[1152,128]{0,1:T(8,128)}, f32[1152,256]{0,1:T(8,128)})) %all-reduce.20.cloned.1.call-update) | async-done | bytes 1769488 | tf_op jit(solution)/shard_map/psum | solution.py:139
  571.5 1.4 constant_dynamic-slice_fusion.3
  572.9 1.4 constant_dynamic-slice_fusion.1
  (200 shorter events, 22.9 us)
Async XLA Ops:
  7.2 13.1 %copy-start = (bf16[1,1,256,256]{3,2,1,0:T(8,128)(2,1)S(1)}, bf16[1,1,256,256]{3,2,1,0:T(8,128)(2,1)}, u32[]{:S(2)}) copy-start(bf16[1,1,256,256]{3,2,1,0:T(8,128)(2,1)} %param.15) | copy-start | bytes 393220
  7.2 13.1 %copy-start.1 = (bf16[3,3,128,256]{3,2,1,0:T(8,128)(2,1)S(1)}, bf16[3,3,128,256]{3,2,1,0:T(8,128)(2,1)}, u32[]{:S(2)}) copy-start(bf16[3,3,128,256]{3,2,1,0:T(8,128)(2,1)} %param.13) | copy-start | bytes 1769476
  7.2 564.4 %all-reduce.20.cloned.1.call-start = ((), (), s32[]{:S(2)}) async-start(), calls=%async_computation | async-start | bytes 3538944 | tf_op jit(solution)/shard_map/psum | solution.py:139
  9.1 20.0 %collective-permute-start = (bf16[1,512,128]{1,2,0:T(8,128)(2,1)}, bf16[1,512,128]{1,2,0:T(8,128)(2,1)S(1)}, u32[]{:S(2)}, u32[]{:S(2)}) collective-permute-start(bf16[1,512,128]{1,2,0:T(8,128)(2,1)} %get-tuple-element.60), channel_id=1, source_target_pairs={{0,32},{32,64},{64,96},{96,128},{128,160},{160,192},{192,224},{224... | collective-permute-start | bytes 393224 | tf_op jit(solution)/shard_map/ppermute | solution.py:14
  13.7 15.4 %collective-permute-start.1 = (bf16[1,512,128]{1,2,0:T(8,128)(2,1)}, bf16[1,512,128]{1,2,0:T(8,128)(2,1)}, u32[]{:S(2)}, u32[]{:S(2)}) collective-permute-start(bf16[1,512,128]{1,2,0:T(8,128)(2,1)} %get-tuple-element.61), channel_id=1, source_target_pairs={{32,0},{64,32},{96,64},{128,96},{160,128},{192,160},{224,192},{256... | collective-permute-start | bytes 393224 | tf_op jit(solution)/shard_map/ppermute | solution.py:17
  25.5 6.2 %copy-start.5 = (f32[1,512,128]{1,2,0:T(8,128)}, f32[1,512,128]{1,2,0:T(8,128)S(1)}, u32[]{:S(2)}) copy-start(f32[1,512,128]{1,2,0:T(8,128)S(1)} %get-tuple-element.38) | copy-start | bytes 786436
  25.5 77.5 %collective-permute-start.3 = (f32[512,128]{0,1:T(8,128)}, f32[512,128]{0,1:T(8,128)}, u32[]{:S(2)}, u32[]{:S(2)}) collective-permute-start(f32[512,128]{0,1:T(8,128)} %get-tuple-element.37), channel_id=1, source_target_pairs={{32,0},{64,32},{96,64},{128,96},{160,128},{192,160},{224,192},{256... | collective-permute-start | bytes 786440 | tf_op jit(solution)/shard_map/ppermute | solution.py:25
  40.4 2.3 copy-start.9
  40.4 2.3 copy-start.22
  41.4 1.5 copy-start.20
  42.6 1.0 copy-start.3
  42.9 1.0 copy-start.19
  43.6 1.0 copy-start.18
  43.9 1.0 copy-start.13
  44.6 1.0 copy-start.14
  44.6 1.0 copy-start.37
  71.7 32.8 %copy-start.12 = (f32[1,512,32,4]{1,0,3,2:T(1,128)S(1)}, f32[1,512,32,4]{1,0,3,2:T(1,128)}, u32[]{:S(2)}) copy-start(f32[1,512,32,4]{1,0,3,2:T(1,128)} %concatenate.65) | copy-start | bytes 786436
  104.9 0.7 copy-start.38
  105.0 0.7 copy-start.41
  105.1 29.9 %copy-start.6 = (f32[1,512,128]{1,2,0:T(8,128)S(1)}, f32[1,512,128]{1,2,0:T(8,128)}, u32[]{:S(2)}) copy-start(f32[1,512,128]{1,2,0:T(8,128)} %copy-done.5) | copy-start | bytes 786436
  105.6 29.3 %copy-start.7 = (f32[2,512,128]{1,2,0:T(8,128)S(1)}, f32[2,512,128]{1,2,0:T(8,128)}, u32[]{:S(2)}) copy-start(f32[2,512,128]{1,2,0:T(8,128)} %copy.44) | copy-start | bytes 1572868
  142.7 1.4 copy-start.39
  142.7 1.4 copy-start.40
  142.9 1.4 copy-start.42
  143.0 103.7 %copy-start.4 = (bf16[1,2,512,128]{3,2,1,0:T(8,128)(2,1)S(1)}, bf16[1,2,512,128]{3,2,1,0:T(8,128)(2,1)}, u32[]{:S(2)}) copy-start(bf16[1,2,512,128]{3,2,1,0:T(8,128)(2,1)} %param.8) | copy-start | bytes 786436
  144.1 102.8 %copy-start.8 = (bf16[2,512,128]{1,2,0:T(8,128)(2,1)S(1)}, bf16[2,512,128]{1,2,0:T(8,128)(2,1)}, u32[]{:S(2)}) copy-start(bf16[2,512,128]{1,2,0:T(8,128)(2,1)} %get-tuple-element.52) | copy-start | bytes 786436
  144.1 107.9 %copy-start.35 = (f32[1,128,128]{2,1,0:T(8,128)S(1)}, f32[1,128,128]{2,1,0:T(8,128)}, u32[]{:S(2)}) copy-start(f32[1,128,128]{2,1,0:T(8,128)} %convolution_bitcast_fusion.23) | copy-start | bytes 196612
  144.1 107.9 %copy-start.36 = (f32[1,128,128]{2,1,0:T(8,128)S(1)}, f32[1,128,128]{2,1,0:T(8,128)}, u32[]{:S(2)}) copy-start(f32[1,128,128]{2,1,0:T(8,128)} %convolution_bitcast_fusion.24) | copy-start | bytes 196612
  144.3 108.8 %copy-start.33 = (f32[1,128,128]{2,1,0:T(8,128)S(1)}, f32[1,128,128]{2,1,0:T(8,128)}, u32[]{:S(2)}) copy-start(f32[1,128,128]{2,1,0:T(8,128)} %convolution_bitcast_fusion.22) | copy-start | bytes 196612
  144.3 108.8 %copy-start.34 = (f32[1,128,128]{2,1,0:T(8,128)S(1)}, f32[1,128,128]{2,1,0:T(8,128)}, u32[]{:S(2)}) copy-start(f32[1,128,128]{2,1,0:T(8,128)} %convolution_bitcast_fusion.21) | copy-start | bytes 196612
  247.6 5.8 %copy-start.31 = (f32[1,128,128]{2,1,0:T(8,128)S(1)}, f32[1,128,128]{2,1,0:T(8,128)}, u32[]{:S(2)}) copy-start(f32[1,128,128]{2,1,0:T(8,128)} %convolution_bitcast_fusion.25) | copy-start | bytes 196612
  247.6 5.8 %copy-start.32 = (f32[1,128,128]{2,1,0:T(8,128)S(1)}, f32[1,128,128]{2,1,0:T(8,128)}, u32[]{:S(2)}) copy-start(f32[1,128,128]{2,1,0:T(8,128)} %convolution_bitcast_fusion.26) | copy-start | bytes 196612
  247.6 12.7 %collective-permute-start.2 = (bf16[512,128]{0,1:T(8,128)(2,1)}, bf16[512,128]{0,1:T(8,128)(2,1)}, u32[]{:S(2)}, u32[]{:S(2)}) collective-permute-start(bf16[512,128]{0,1:T(8,128)(2,1)} %slice_bitcast_fusion.1), channel_id=1, source_target_pairs={{0,32},{32,64},{64,96},{96,128},{128,160},{160,192},{192,224},{224... | collective-permute-start | bytes 393224 | tf_op jit(solution)/shard_map/ppermute | solution.py:25
  254.6 28.5 %copy-start.2 = (bf16[3,3,128,256]{3,2,1,0:T(8,128)(2,1)S(1)}, bf16[3,3,128,256]{3,2,1,0:T(8,128)(2,1)}, u32[]{:S(2)}) copy-start(bf16[3,3,128,256]{3,2,1,0:T(8,128)(2,1)} %param.13) | copy-start | bytes 1769476
  254.6 32.4 %collective-permute-start.4 = (bf16[1,512,128]{1,2,0:T(8,128)(2,1)}, bf16[1,512,128]{1,2,0:T(8,128)(2,1)}, u32[]{:S(2)}, u32[]{:S(2)}) collective-permute-start(bf16[1,512,128]{1,2,0:T(8,128)(2,1)} %get-tuple-element.56), channel_id=1, source_target_pairs={{0,32},{32,64},{64,96},{96,128},{128,160},{160,192},{192,224},{224... | collective-permute-start | bytes 393224 | tf_op jit(solution)/shard_map/ppermute | solution.py:14
  256.6 30.4 %collective-permute-start.5 = (bf16[1,512,128]{1,2,0:T(8,128)(2,1)}, bf16[1,512,128]{1,2,0:T(8,128)(2,1)}, u32[]{:S(2)}, u32[]{:S(2)}) collective-permute-start(bf16[1,512,128]{1,2,0:T(8,128)(2,1)} %get-tuple-element.57), channel_id=1, source_target_pairs={{32,0},{64,32},{96,64},{128,96},{160,128},{192,160},{224,192},{256... | collective-permute-start | bytes 393224 | tf_op jit(solution)/shard_map/ppermute | solution.py:17
  266.1 18.2 %copy-start.23 = (bf16[1,256,128]{1,2,0:T(8,128)(2,1)}, bf16[1,256,128]{1,2,0:T(8,128)(2,1)S(1)}, u32[]{:S(2)}) copy-start(bf16[1,256,128]{1,2,0:T(8,128)(2,1)S(1)} %slice.253) | copy-start | bytes 196612
  268.5 15.7 %copy-start.25 = (bf16[1,256,128]{1,2,0:T(8,128)(2,1)}, bf16[1,256,128]{1,2,0:T(8,128)(2,1)S(1)}, u32[]{:S(2)}) copy-start(bf16[1,256,128]{1,2,0:T(8,128)(2,1)S(1)} %slice.251) | copy-start | bytes 196612
  270.9 13.1 %copy-start.27 = (bf16[1,256,128]{1,2,0:T(8,128)(2,1)}, bf16[1,256,128]{1,2,0:T(8,128)(2,1)S(1)}, u32[]{:S(2)}) copy-start(bf16[1,256,128]{1,2,0:T(8,128)(2,1)S(1)} %slice.249) | copy-start | bytes 196612
  283.0 1.4 copy-start.29
  291.6 2.2 copy-start.10
  292.6 1.4 copy-start.16
  294.1 1.0 copy-start.21
  295.3 1.0 copy-start.17
  296.2 0.9 copy-start.15
  297.4 1.0 copy-start.11
  297.6 0.9 copy-start.28
  297.7 1.9 copy-start.26
  298.4 1.4 copy-start.24
  298.7 1.5 copy-start.30
  298.7 1.5 copy-start.43
Sparse Core Ops, SparseCore 0:
  297.8 273.7 all-reduce.19
where the time goes:
time: 582 us; the launch traced here: 581 us
  waiting for transfers between devices  270 us (46%)
  blocking collectives  184 us (32%)
  local copies, waits for them, and re-layouts  57.4 us (10%)
  starting transfers between devices  21.5 us (4%)
  matrix products  19.1 us (3%)
  between operations  15.3 us (3%)
  other arithmetic  13.4 us (2%)
    psum x1, waiting for transfers between devices, shards(): lax.psum((conv_pack, small_pack, down_pack, bias_pack), ('rows', 'dp'))  270 us
    psum x1, blocking collectives, shards(): lax.psum((conv_pack, small_pack, down_pack, bias_pack), ('rows', 'dp'))  102 us
    psum x1, blocking collectives, shards(): var = lax.psum(jnp.sum(centred * centred, axis=(0, 1, 3)), 'rows') / count  30 us
    psum x1, blocking collectives, shards(): lax.psum((jnp.sum(scaled, axis=(0, 1, 3)), jnp.sum(scaled * normed_g, axi...  27.1 us
    psum x1, blocking collectives, shards(): mean = lax.psum(jnp.sum(grouped, axis=(0, 1, 3)), 'rows') / count  25.3 us
    slice x9, local copies, waits for them, and re-layouts, shards(): shifted[kh:kh + 2 * half_rows:2, kw:kw + 2 * half_cols:2]  21.5 us
  transfers between devices with their start and end apart: 7, of which 1 were waited for; matrix products, arithmetic and copies ran while one was open for 10% of the time, Pallas kernels for 0%

commit v1 on v0

v1 whole, which is shorter than its diff:
```python
import jax
import jax.numpy as jnp
from jax import lax
from jax.experimental import pallas as pl
from jax.experimental.pallas import tpu as pltpu
from jax.sharding import PartitionSpec as P

GROUPS = 32
CHANS = 128
OUTS = 256
BF = jnp.bfloat16
F32 = jnp.float32
MESH = pl.DeviceIdType.MESH
EPS = 1e-05
DOWN_CHUNKS = 9
PAIRS = 7


def nn(a, b):
    return lax.dot_general(a, b, (((1,), (0,)), ((), ())), preferred_element_type=F32)


def nt(a, b):
    return lax.dot_general(a, b, (((1,), (1,)), ((), ())), preferred_element_type=F32)


def tn(a, b):
    return lax.dot_general(a, b, (((0,), (0,)), ((), ())), preferred_element_type=F32)


def group_sum(x):
    lane = lax.broadcasted_iota(jnp.int32, x.shape, 1)
    x = x + jnp.where(lane % 2 == 0, pltpu.roll(x, CHANS - 1, 1), pltpu.roll(x, 1, 1))
    return x + jnp.where(lane % 4 < 2, pltpu.roll(x, CHANS - 2, 1), pltpu.roll(x, 2, 1))


def twice(x):
    return jnp.concatenate([x, x], axis=1)


def fold(x):
    return x[:, :CHANS] + x[:, CHANS:]


def kernel(
    rows_n,
    dp_n,
    img,
    cw,
    cb,
    gain_ref,
    shift_ref,
    dw,
    db,
    cot,
    block_out,
    gimg_out,
    gout,
    wide,
    tall,
    edge_img,
    edge_cot,
    x4,
    m4,
    g4,
    wf,
    wb,
    hid,
    gpre,
    gmix,
    stat_a,
    stat_b,
    mine,
    full,
    cs,
    cr,
    rs,
    rr,
    red,
    dr,
    img_s,
    img_r,
    cot_s,
    cot_r,
    mix_s,
    mix_r,
    g_s,
    g_r,
    sa_s,
    sa_r,
    sb_s,
    sb_r,
    c_s,
    c_r,
    r_s,
    r_r,
    d_s,
    d_r,
    o_s,
    o_r,
):
    r = lax.axis_index("rows")
    d = lax.axis_index("dp")
    core = lax.rem(r, 2)
    slot = lax.div(r, 2)
    mate = r + 1 - 2 * core
    half = cot.shape[1]
    cols = 2 * half
    n_local = float(2 * cols * (CHANS // GROUPS))
    n_total = n_local * rows_n
    last = rows_n - 1
    slots = rows_n // 2

    def remote(src, dst, send, recv, **where):
        return pltpu.make_async_remote_copy(
            src_ref=src,
            dst_ref=dst,
            send_sem=send,
            recv_sem=recv,
            device_id=where,
            device_id_type=MESH,
        )

    barrier = pltpu.get_barrier_semaphore()

    def greet_row(i, c):
        pl.semaphore_signal(
            barrier, inc=1, device_id={"rows": lax.rem(r + i, rows_n)}, device_id_type=MESH
        )
        return c

    def greet_dp(i, c):
        pl.semaphore_signal(
            barrier, inc=1, device_id={"dp": lax.rem(d + i, dp_n)}, device_id_type=MESH
        )
        return c

    lax.fori_loop(1, rows_n, greet_row, 0)
    lax.fori_loop(1, dp_n, greet_dp, 0)

    zero_block = jnp.zeros((CHANS, CHANS), BF)
    for kh in range(3):
        for kw in range(3):
            tap = cw[kh, kw]
            wf[kh, kw * CHANS : (kw + 1) * CHANS, :CHANS] = tap
            wf[kh, (kw + 1) * CHANS : (kw + 2) * CHANS, CHANS:] = tap
            wb[kh, :CHANS, (2 - kw) * CHANS : (3 - kw) * CHANS] = tap
            wb[kh, CHANS:, (3 - kw) * CHANS : (4 - kw) * CHANS] = tap
        wf[kh, 3 * CHANS :, :CHANS] = zero_block
        wf[kh, :CHANS, CHANS:] = zero_block
        wb[kh, :CHANS, 3 * CHANS :] = zero_block
        wb[kh, CHANS:, :CHANS] = zero_block

    tall[:8, :] = jnp.zeros((8, CHANS), F32)
    tall[cols + 8 :, :] = jnp.zeros((8, CHANS), F32)
    wide[:8, :] = jnp.zeros((8, OUTS), F32)
    wide[half + 8 :, :] = jnp.zeros((8, OUTS), F32)

    def split_columns(row, f):
        tall[8 : cols + 8, :] = row.astype(F32)
        for k, start in enumerate((7, 8, 9, 10)):
            x4[f, :, k * CHANS : (k + 1) * CHANS] = tall[pl.ds(start, half, stride=2), :].astype(BF)

    def shifted(x, by):
        width = x.shape[1]
        wide[8 : half + 8, :width] = x
        return wide[8 + by : half + 8 + by, :width]

    @pl.when(r == 0)
    def _():
        edge_img[0] = jnp.zeros(edge_img.shape[1:], BF)
        m4[0] = jnp.zeros(m4.shape[1:], BF)
        g4[0] = jnp.zeros(g4.shape[1:], BF)

    @pl.when(r == last)
    def _():
        edge_img[1] = jnp.zeros(edge_img.shape[1:], BF)
        edge_cot[...] = jnp.zeros(edge_cot.shape, BF)
        g4[3] = jnp.zeros(g4.shape[1:], BF)

    pl.semaphore_wait(barrier, rows_n + dp_n - 2)
    up = lax.max(r - 1, 0)
    down = lax.min(r + 1, last)
    img_down = remote(img.at[0, 1], edge_img.at[0], img_s.at[0], img_r.at[0], rows=down)
    img_up = remote(img.at[0, 0], edge_img.at[1], img_s.at[1], img_r.at[1], rows=up)
    cot_up = remote(cot.at[0], edge_cot, cot_s, cot_r, rows=up)
    mix_down = remote(m4.at[2], m4.at[0], mix_s, mix_r, rows=down)
    mid = pl.ds(CHANS, 2 * CHANS)
    g_down = remote(g4.at[2, :, mid], g4.at[0, :, mid], g_s.at[0], g_r.at[0], rows=down)
    g_up = remote(g4.at[1, :, mid], g4.at[3, :, mid], g_s.at[1], g_r.at[1], rows=up)

    @pl.when(r < last)
    def _():
        img_down.start()

    @pl.when(r > 0)
    def _():
        img_up.start()
        cot_up.start()

    for a in range(2):
        split_columns(img[0, a], a + 1)

    bias = twice(cb[...])
    hid[0] = nn(x4[1], wf[1]) + nn(x4[2], wf[2]) + bias
    hid[1] = nn(x4[1], wf[0]) + nn(x4[2], wf[1]) + bias

    @pl.when(r > 0)
    def _():
        img_down.wait_recv()

    split_columns(edge_img[0], 0)
    hid[0] += nn(x4[0], wf[0])

    @pl.when(r < last)
    def _():
        img_up.wait_recv()

    split_columns(edge_img[1], 3)
    hid[1] += nn(x4[3], wf[2])

    def spread(table, send, recv):
        def go(i, c):
            to = lax.rem(r + i, rows_n)
            remote(table.at[r], table.at[r], send.at[to], recv.at[r], rows=to).start()
            return c

        lax.fori_loop(1, rows_n, go, 0)

    def gathered(table, send, recv):
        def go(i, c):
            other = lax.rem(r + i, rows_n)
            remote(table.at[other], table.at[other], send.at[other], recv.at[other], rows=other).wait()
            return c

        lax.fori_loop(1, rows_n, go, 0)

    def colsum(x):
        return jnp.sum(x, axis=0, keepdims=True)

    own_sum = fold(colsum(hid[0]) + colsum(hid[1]))
    own_mean = twice(group_sum(jnp.broadcast_to(own_sum, (8, CHANS)))[:1] / n_local)
    off0 = hid[0] - own_mean
    off1 = hid[1] - own_mean
    own_sq = fold(colsum(off0 * off0) + colsum(off1 * off1))
    stat_a[r, 0:1, :] = own_sum
    stat_a[r, 1:2, :] = own_sq
    stat_a[r, 2:8, :] = jnp.zeros((6, CHANS), F32)
    spread(stat_a, sa_s, sa_r)

    @pl.when(r < last)
    def _():
        cot_up.wait_recv()

    def pull(grad, lead, kh):
        both = dw[kh, 1:3].reshape(2 * CHANS, OUTS)
        return nt(grad, both), nt(lead, dw[kh, 0])

    own_cot = cot[0]
    own_cot32 = own_cot.astype(F32)
    cot_sum = colsum(own_cot32)
    lead_cot = shifted(own_cot32, 1).astype(BF)
    whole, odd = pull(own_cot, lead_cot, 1)
    gmix[0] = whole
    gmix[0, :, CHANS:] += odd
    whole, odd = pull(own_cot, lead_cot, 2)
    gmix[1] = whole
    gmix[1, :, CHANS:] += odd
    below = edge_cot[...]
    whole, odd = pull(below, shifted(below.astype(F32), 1).astype(BF), 0)
    gmix[1] += whole
    gmix[1, :, CHANS:] += odd

    gathered(stat_a, sa_s, sa_r)
    table = stat_a[...]
    groups = group_sum(table.reshape(rows_n * 8, CHANS)).reshape(rows_n, 8, CHANS)
    group_tot = jnp.sum(groups, axis=0)
    mean = group_tot[0:1] / n_total
    dev = groups / n_local - mean.reshape(1, 1, CHANS)
    spread_sq = jnp.sum(dev * dev, axis=0)[0:1] * n_local
    rstd = lax.rsqrt((group_tot[1:2] + spread_sq) / n_total + EPS)
    channel_sum = jnp.sum(table, axis=0)[0:1]
    mean2, rstd2 = twice(mean), twice(rstd)
    gain2, shift2 = twice(gain_ref[...]), twice(shift_ref[...])

    sum_gp = jnp.zeros((1, 2 * CHANS), F32)
    sum_gpn = jnp.zeros((1, 2 * CHANS), F32)
    for a in (1, 0):
        normed = (hid[a] - mean2) * rstd2
        pre = normed * gain2 + shift2
        sig = jax.nn.sigmoid(pre)
        mixed = (x4[a + 1, :, CHANS : 3 * CHANS].astype(F32) + pre * sig).astype(BF)
        m4[a + 1, :, CHANS:] = mixed
        m4[a + 1, :, :CHANS] = shifted(mixed[:, CHANS:].astype(F32), -1).astype(BF)
        if a == 1:

            @pl.when(r < last)
            def _():
                mix_down.start()

        gp = gmix[a] * sig * (1.0 + pre * (1.0 - sig))
        hid[a] = normed
        gpre[a] = gp
        sum_gp += colsum(gp)
        sum_gpn += colsum(gp * normed)

    stat_b[r, 0:1, :] = fold(sum_gp)
    stat_b[r, 1:2, :] = fold(sum_gpn)
    stat_b[r, 2:3, :] = cot_sum[:, :CHANS]
    stat_b[r, 3:4, :] = cot_sum[:, CHANS:]
    stat_b[r, 4:8, :] = jnp.zeros((4, CHANS), F32)
    spread(stat_b, sb_s, sb_r)

    def down_grad(kh):
        part = tn(own_cot, m4[kh])
        for kw in range(3):
            c = 3 * kh + kw
            full[c % 2, c // 2] = part[:, kw * CHANS : (kw + 1) * CHANS]

    def taps(kh):
        return dw[kh].reshape(3 * CHANS, OUTS)

    out = nn(m4[1], taps(1)) + nn(m4[2], taps(2)) + db[...]
    down_grad(1)
    down_grad(2)

    @pl.when(r > 0)
    def _():
        mix_down.wait_recv()

    down_grad(0)
    cs[0:4] = full[1 - core, 0:4].astype(BF)
    pair_one = remote(cs.at[0:4], cr.at[0:4], c_s.at[0], c_r.at[0], rows=mate)
    pair_two = remote(cs.at[4:PAIRS], cr.at[4:PAIRS], c_s.at[1], c_r.at[1], rows=mate)
    pair_one.start()
    block_out[0, 0] = (out + nn(m4[0], taps(0))).astype(BF)

    gathered(stat_b, sb_s, sb_r)
    totals = jnp.sum(stat_b[...], axis=0)
    tot_gp = totals[0:1]
    tot_gpn = totals[1:2]
    means = group_sum(
        jnp.broadcast_to(gain_ref[...], (8, CHANS)) * totals
    ) / n_total
    m1, m2 = means[0:1], means[1:2]
    m1w, m2w = twice(m1), twice(m2)
    for a in range(2):
        grad = (rstd2 * (gpre[a] * gain2 - m1w - hid[a] * m2w)).astype(BF)
        g4[a + 1, :, CHANS : 3 * CHANS] = grad

    @pl.when(r < last)
    def _():
        g_down.start()

    @pl.when(r > 0)
    def _():
        g_up.start()

    n_channel = float(2 * cols * rows_n)
    tot_normed = (channel_sum - n_channel * mean) * rstd
    tot_bias = rstd * (gain_ref[...] * tot_gp - n_channel * m1 - m2 * tot_normed)
    mine[0:1, :] = tot_bias
    mine[1:2, :] = tot_gpn
    mine[2:3, :] = tot_gp
    mine[3:4, :] = totals[2:3]
    mine[4:5, :] = totals[3:4]
    mine[5:8, :] = jnp.zeros((3, CHANS), F32)

    def row_send(low, high):
        for i in range(1, slots):
            to = lax.rem(slot + i, slots)

            @pl.when((to >= low) & (to < high))
            def _():
                remote(
                    rs.at[lax.min(to, PAIRS - 1)],
                    rr.at[slot],
                    r_s.at[to],
                    r_r.at[slot],
                    rows=2 * to + core,
                ).start()

    def pair_sum(low, high):
        for k in range(low, high):
            both = full[core, k] + cr[k].astype(F32)
            full[core, k] = both
            rs[k] = both.astype(BF)
        row_send(low, high)

    pair_one.wait()
    pair_sum(0, 4)

    sub = lax.broadcasted_iota(jnp.int32, (CHANS, CHANS), 0) % 8
    conv_taps = []
    for kh in range(3):
        part = tn(g4[1, :, CHANS : 3 * CHANS], x4[kh]) + tn(
            g4[2, :, CHANS : 3 * CHANS], x4[kh + 1]
        )
        for kw in range(3):
            conv_taps.append(
                part[:CHANS, kw * CHANS : (kw + 1) * CHANS]
                + part[CHANS:, (kw + 1) * CHANS : (kw + 2) * CHANS]
            )
    conv_taps.append(jnp.zeros((CHANS, CHANS), F32))
    for k in range(5):
        c = DOWN_CHUNKS + k
        one, two = conv_taps[2 * k], conv_taps[2 * k + 1]
        full[c % 2, c // 2, :CHANS] = jnp.where(sub < 4, one, pltpu.roll(two, 4, 0))
        full[c % 2, c // 2, CHANS:] = jnp.where(sub < 4, pltpu.roll(one, CHANS - 4, 0), two)
    cs[4:PAIRS] = full[1 - core, 4:PAIRS].astype(BF)
    pair_two.start()

    def sides(f):
        grad = g4[f, :, CHANS : 3 * CHANS].astype(F32)
        g4[f, :, :CHANS] = shifted(grad[:, CHANS:], -1).astype(BF)
        g4[f, :, 3 * CHANS :] = shifted(grad[:, :CHANS], 1).astype(BF)

    sides(1)
    sides(2)
    gmix[0] += nt(g4[1], wb[1]) + nt(g4[2], wb[0])
    gmix[1] += nt(g4[1], wb[2]) + nt(g4[2], wb[1])

    pair_two.wait()
    pair_sum(4, PAIRS)

    def put_row(a):
        tall[pl.ds(8, half, stride=2), :] = gmix[a, :, :CHANS]
        tall[pl.ds(9, half, stride=2), :] = gmix[a, :, CHANS:]
        gimg_out[0, a] = tall[8 : cols + 8, :].astype(BF)

    @pl.when(r > 0)
    def _():
        g_down.wait_recv()
        sides(0)

    gmix[0] += nt(g4[0], wb[2])
    put_row(0)

    @pl.when(r < last)
    def _():
        g_up.wait_recv()
        sides(3)

    gmix[1] += nt(g4[3], wb[0])
    put_row(1)

    @pl.when(slot < PAIRS)
    def _():
        def take(i, total):
            other = lax.rem(slot + i, slots)
            remote(
                rs.at[0], rr.at[other], r_s.at[other], r_r.at[other], rows=2 * other + core
            ).wait_recv()
            return total + rr[other].astype(F32)

        red[...] = lax.fori_loop(1, slots, take, full[core, lax.min(slot, PAIRS - 1)])

    @pl.when(slot == PAIRS)
    def _():
        red[...] = jnp.broadcast_to(mine[...][None], (32, 8, CHANS)).reshape(256, CHANS)

    def place(e):
        row = jnp.where(r < DOWN_CHUNKS, e, lax.rem(e, 2) * 16 + lax.div(e, 2))
        return pl.ds(pl.multiple_of(row * 8, 8), 8)

    def to_owner(i, c):
        to = lax.rem(d + i, dp_n)
        remote(red.at[place(to)], dr.at[d], d_s.at[to], d_r.at[d], dp=to).start()
        return c

    lax.fori_loop(1, dp_n, to_owner, 0)
    dr[d] = red[place(d), :]

    def from_peer(i, c):
        other = lax.rem(d + i, dp_n)
        remote(red.at[place(other)], dr.at[other], d_s.at[other], d_r.at[other], dp=other).wait()
        return c

    lax.fori_loop(1, dp_n, from_peer, 0)
    gout[r] = jnp.sum(dr[...], axis=0)
    spread(gout, o_s, o_r)
    gathered(gout, o_s, o_r)

    @pl.when(r < last)
    def _():
        img_down.wait_send()
        mix_down.wait_send()
        g_down.wait_send()

    @pl.when(r > 0)
    def _():
        img_up.wait_send()
        cot_up.wait_send()
        g_up.wait_send()

    for i in range(1, slots):
        to = lax.rem(slot + i, slots)

        @pl.when(to < PAIRS)
        def _():
            remote(rs.at[0], rr.at[slot], r_s.at[to], r_r.at[slot], rows=2 * to + core).wait_send()


def shards(
    images, conv_weight, conv_bias, norm_gain, norm_shift, down_weight, down_bias, cotangent
):
    rows_n = lax.axis_size("rows")
    dp_n = lax.axis_size("dp")
    _, local_rows, cols, chans = images.shape
    half = cols // 2
    vmem = pl.BlockSpec(memory_space=pltpu.VMEM)
    dma = pltpu.SemaphoreType.DMA
    scratch = [
        pltpu.VMEM((half + 16, OUTS), F32),
        pltpu.VMEM((cols + 16, CHANS), F32),
        pltpu.VMEM((2, cols, CHANS), BF),
        pltpu.VMEM((half, OUTS), BF),
        pltpu.VMEM((4, half, 4 * CHANS), BF),
        pltpu.VMEM((3, half, 3 * CHANS), BF),
        pltpu.VMEM((4, half, 4 * CHANS), BF),
        pltpu.VMEM((3, 4 * CHANS, 2 * CHANS), BF),
        pltpu.VMEM((3, 2 * CHANS, 4 * CHANS), BF),
        pltpu.VMEM((2, half, 2 * CHANS), F32),
        pltpu.VMEM((2, half, 2 * CHANS), F32),
        pltpu.VMEM((2, half, 2 * CHANS), F32),
        pltpu.VMEM((rows_n, 8, CHANS), F32),
        pltpu.VMEM((rows_n, 8, CHANS), F32),
        pltpu.VMEM((8, CHANS), F32),
        pltpu.VMEM((2, PAIRS, OUTS, CHANS), F32),
        pltpu.VMEM((PAIRS, OUTS, CHANS), BF),
        pltpu.VMEM((PAIRS, OUTS, CHANS), BF),
        pltpu.VMEM((PAIRS, OUTS, CHANS), BF),
        pltpu.VMEM((rows_n // 2, OUTS, CHANS), BF),
        pltpu.VMEM((OUTS, CHANS), F32),
        pltpu.VMEM((dp_n, 8, CHANS), F32),
        dma((2,)),
        dma((2,)),
        dma,
        dma,
        dma,
        dma,
        dma((2,)),
        dma((2,)),
        dma((rows_n,)),
        dma((rows_n,)),
        dma((rows_n,)),
        dma((rows_n,)),
        dma((2,)),
        dma((2,)),
        dma((rows_n // 2,)),
        dma((rows_n // 2,)),
        dma((dp_n,)),
        dma((dp_n,)),
        dma((rows_n,)),
        dma((rows_n,)),
    ]

    def body(*refs):
        kernel(rows_n, dp_n, *refs)

    block, grad_image, table = pl.pallas_call(
        body,
        out_shape=(
            jax.ShapeDtypeStruct((1, 1, half, OUTS), BF),
            jax.ShapeDtypeStruct((1, local_rows, cols, chans), BF),
            jax.ShapeDtypeStruct((rows_n, 8, CHANS), F32),
        ),
        in_specs=[vmem] * 8,
        out_specs=(vmem, vmem, vmem),
        scratch_shapes=scratch,
        compiler_params=pltpu.CompilerParams(
            collective_id=0, has_side_effects=True, vmem_limit_bytes=40 * 1024 * 1024
        ),
        name="step",
    )(
        images,
        conv_weight,
        conv_bias.reshape(1, CHANS),
        norm_gain.reshape(1, CHANS),
        norm_shift.reshape(1, CHANS),
        down_weight,
        down_bias.reshape(1, OUTS),
        cotangent.reshape(1, half, OUTS),
    )
    d = lax.axis_index("dp")
    down_part = jnp.swapaxes(table[:DOWN_CHUNKS], 1, 2).reshape(3, 3, CHANS, 8)
    conv_part = jnp.swapaxes(
        table[DOWN_CHUNKS:14].reshape(10, 4, CHANS)[:9], 1, 2
    ).reshape(3, 3, CHANS, 4)
    vectors = table[14]
    narrow = lax.dynamic_slice(vectors, (0, 4 * d), (3, 4))
    wide = lax.dynamic_slice(vectors[3:5].reshape(OUTS), (8 * d,), (8,))
    return block, grad_image, conv_part, narrow[0], narrow[1], narrow[2], down_part, wide


def solution(mesh):
    spread = P("dp", "rows", None, None)
    in_specs = (spread, P(), P(), P(), P(), P(), P(), spread)
    out_specs = (
        spread,
        spread,
        P(None, None, None, "dp"),
        P("dp"),
        P("dp"),
        P("dp"),
        P(None, None, None, "dp"),
        P("dp"),
    )
    return jax.shard_map(shards, mesh=mesh, in_specs=in_specs, out_specs=out_specs, check_vma=False)
```

time: 582 us -> 66.1 us (0.11)
  waiting for transfers between devices: 270 us -> 0 us
  blocking collectives: 184 us -> 0 us
  Pallas kernels: 0 us -> 56.8 us
  local copies, waits for them, and re-layouts: 57.4 us -> 8.34 us
  starting transfers between devices: 21.5 us -> 0 us
  matrix products: 19.1 us -> 0 us
  between operations: 15.3 us -> 0.7 us
  other arithmetic: 13.4 us -> 0 us
    psum x1 -> x0, waiting for transfers between devices: 270 us -> none  [shards(): lax.psum((conv_pack, small_pack, down_pack, bias_pack), ('rows', 'dp'))]
    psum x4 -> x0, blocking collectives: 184 us -> none  [the longest x1 102 us: shards(): lax.psum((conv_pack, small_pack, down_pack, bias_pack), ('rows', 'dp'))]
    pallas_call x0 -> x1, Pallas kernels: none -> 56.8 us  [shards(): pl.pallas_call(body, out_shape=(jax.ShapeDtypeStruct((1, 1, half, OUTS),...]
    slice x29 -> x4, local copies, waits for them, and re-layouts: 36.3 us -> 1.23 us  [the longest x1 0.62 us: shards(): down_part = jnp.swapaxes(table[:DOWN_CHUNKS], 1, 2).reshape(3, 3, CHANS, 8)]
    ppermute x6 -> x0, starting transfers between devices: 21.4 us -> none  [the longest x2 8.52 us: extended(): lax.ppermute(lax.slice_in_dim(block, 0, width, axis=dim), axis, backward)]
    dot_general x54 -> x0, matrix products: 19.1 us -> none  [the longest x9 6.88 us: shards(): line.append(jnp.dot(piece.T, flat, preferred_element_type=jnp.float32))]
  transfers between devices with their start and end apart: 7 -> 0, of which waited for: 1 -> 0; matrix products, arithmetic and copies ran while one was open for 10% -> 0% of each run, Pallas kernels for 0% -> 0%
where the time goes in v1:
time: 66.1 us; the launch traced here: 65.8 us
  Pallas kernels  56.8 us (86%)
  local copies, waits for them, and re-layouts  8.34 us (13%)
  between operations  0.7 us (1%)
    pallas_call x1, Pallas kernels, shards(): pl.pallas_call(body, out_shape=(jax.ShapeDtypeStruct((1, 1, half, OUTS),...  56.8 us
    unnamed x18, local copies, waits for them, and re-layouts  5.92 us

profile of v1, /device:TPU:1, one launch (start us, length us, event | category | flops | bytes accessed | tf_op | source)
XLA Modules:
  0.0 65.8 jit_solution(9553740381597964441)
XLA Ops:
  0.6 0.0 copy-start.6
  0.6 0.0 copy-start.7
  0.7 0.0 copy-start.4
  0.7 0.0 copy-start.5
  0.7 0.6 copy-done.6
  1.3 0.0 copy-done.7
  1.3 0.0 copy-done.4
  1.4 0.0 copy-done.5
  1.4 0.0 copy-start
  1.4 1.1 %copy-done = bf16[3,3,128,256]{3,2,1,0:T(8,128)(2,1)S(1)} copy-done((bf16[3,3,128,256]{3,2,1,0:T(8,128)(2,1)S(1)}, bf16[3,3,128,256]{3,2,1,0:T(8,128)(2,1)}, u32[]{:S(2)}) %copy-start) | copy-done | bytes 589848
  2.4 0.0 copy-start.1
  2.4 1.0 %copy-done.1 = bf16[3,3,128,128]{3,2,1,0:T(8,128)(2,1)S(1)} copy-done((bf16[3,3,128,128]{3,2,1,0:T(8,128)(2,1)S(1)}, bf16[3,3,128,128]{3,2,1,0:T(8,128)(2,1)}, u32[]{:S(2)}) %copy-start.1) | copy-done | bytes 294936
  3.4 0.0 copy-start.2
  3.4 0.9 %copy-done.2 = bf16[1,2,512,128]{3,2,1,0:T(8,128)(2,1)S(1)} copy-done((bf16[1,2,512,128]{3,2,1,0:T(8,128)(2,1)S(1)}, bf16[1,2,512,128]{3,2,1,0:T(8,128)(2,1)}, u32[]{:S(2)}) %copy-start.2) | copy-done | bytes 262168
  4.3 0.0 copy-start.3
  4.3 0.9 %copy-done.3 = bf16[1,1,256,256]{3,2,1,0:T(8,128)(2,1)S(1)} copy-done((bf16[1,1,256,256]{3,2,1,0:T(8,128)(2,1)S(1)}, bf16[1,1,256,256]{3,2,1,0:T(8,128)(2,1)}, u32[]{:S(2)}) %copy-start.3) | copy-done | bytes 131096
  5.2 56.8 %step.1 = (bf16[1,1,256,256]{3,2,1,0:T(8,128)(2,1)S(1)}, bf16[1,2,512,128]{3,2,1,0:T(8,128)(2,1)S(1)}, f32[16,8,128]{2,1,0:T(8,128)S(1)}) custom-call(bf16[1,2,512,128]{3,2,1,0:T(8,128)(2,1)S(1)} %copy-done.2, bf16[3,3,128,128]{3,2,1,0:T(8,128)(2,1)S(1)} %copy-done.1, f32[1,128]{1,0:T(1,128)S(1)} %bitcast.22, f32[1,128]{1,0:T(1,128)S(1)} %bitcast.23, ...), custom_call_target="tpu_custom_call" | custom-call | tf_op jit(solution)/shard_map/step/pallas_call | solution.py:561
  62.0 0.6 dynamic_slice.7
  62.6 0.1 constant_dynamic-slice_fusion
  62.7 0.5 slice_bitcast_fusion.1
  63.2 0.6 slice.35
  63.8 0.6 slice.37
  64.4 0.7 copy.18
  65.1 0.7 %copy.19 = bf16[1,2,512,128]{3,2,1,0:T(8,128)(2,1)} copy(bf16[1,2,512,128]{3,2,1,0:T(8,128)(2,1)S(1)} %get-tuple-element.26) | data formatting | bytes 524288
  (3 shorter events, 0.0 us)
Async XLA Ops:
  0.6 0.7 copy-start.6
  0.6 0.7 %copy-start.7 = (f32[128]{0:T(128)S(1)}, f32[128]{0:T(128)}, u32[]{:S(2)}) copy-start(f32[128]{0:T(128)} %param.12) | copy-start | bytes 1540
  0.7 0.7 %copy-start.4 = (f32[256]{0:T(256)S(1)}, f32[256]{0:T(256)}, u32[]{:S(2)}) copy-start(f32[256]{0:T(256)} %param.14) | copy-start | bytes 3076
  0.7 0.7 %copy-start.5 = (f32[128]{0:T(128)S(1)}, f32[128]{0:T(128)}, u32[]{:S(2)}) copy-start(f32[128]{0:T(128)} %param.10) | copy-start | bytes 1540
  1.4 1.1 %copy-start = (bf16[3,3,128,256]{3,2,1,0:T(8,128)(2,1)S(1)}, bf16[3,3,128,256]{3,2,1,0:T(8,128)(2,1)}, u32[]{:S(2)}) copy-start(bf16[3,3,128,256]{3,2,1,0:T(8,128)(2,1)} %refs_5_.1) | copy-start | bytes 1769476
  2.4 1.0 %copy-start.1 = (bf16[3,3,128,128]{3,2,1,0:T(8,128)(2,1)S(1)}, bf16[3,3,128,128]{3,2,1,0:T(8,128)(2,1)}, u32[]{:S(2)}) copy-start(bf16[3,3,128,128]{3,2,1,0:T(8,128)(2,1)} %refs_1_.1) | copy-start | bytes 884740
  3.4 0.9 %copy-start.2 = (bf16[1,2,512,128]{3,2,1,0:T(8,128)(2,1)S(1)}, bf16[1,2,512,128]{3,2,1,0:T(8,128)(2,1)}, u32[]{:S(2)}) copy-start(bf16[1,2,512,128]{3,2,1,0:T(8,128)(2,1)} %refs_0_.1) | copy-start | bytes 786436
  4.3 0.9 %copy-start.3 = (bf16[1,1,256,256]{3,2,1,0:T(8,128)(2,1)S(1)}, bf16[1,1,256,256]{3,2,1,0:T(8,128)(2,1)}, u32[]{:S(2)}) copy-start(bf16[1,1,256,256]{3,2,1,0:T(8,128)(2,1)} %param.15) | copy-start | bytes 393220

commit v2 on v1

--- a/solution.py
+++ b/solution.py
@@ -12,8 +12,8 @@
 F32 = jnp.float32
 MESH = pl.DeviceIdType.MESH
 EPS = 1e-05
-DOWN_CHUNKS = 9
-PAIRS = 7
+TAPS = 9
+LATE = 6
 
 
 def nn(a, b):
@@ -45,6 +45,17 @@
 def kernel(
     rows_n,
     dp_n,
+    img_hbm,
+    cw_hbm,
+    cb_hbm,
+    gain_hbm,
+    shift_hbm,
+    dw_hbm,
+    db_hbm,
+    cot_hbm,
+    block_out,
+    gimg_out,
+    gout,
     img,
     cw,
     cb,
@@ -53,9 +64,8 @@
     dw,
     db,
     cot,
-    block_out,
-    gimg_out,
-    gout,
+    block_v,
+    gimg_v,
     wide,
     tall,
     edge_img,
@@ -71,13 +81,22 @@
     stat_a,
     stat_b,
     mine,
-    full,
+    early,
+    late,
     cs,
     cr,
+    cs2,
+    cr2,
     rs,
     rr,
+    rs2,
+    rr2,
+    red1,
+    red2,
     red,
     dr,
+    load_sem,
+    store_sem,
     img_s,
     img_r,
     cot_s,
@@ -94,6 +113,8 @@
     c_r,
     r_s,
     r_r,
+    q_s,
+    q_r,
     d_s,
     d_r,
     o_s,
@@ -104,7 +125,7 @@
     core = lax.rem(r, 2)
     slot = lax.div(r, 2)
     mate = r + 1 - 2 * core
-    half = cot.shape[1]
+    half = cot.shape[0]
     cols = 2 * half
     n_local = float(2 * cols * (CHANS // GROUPS))
     n_total = n_local * rows_n
@@ -121,23 +142,73 @@
             device_id_type=MESH,
         )
 
+    loads = [
+        pltpu.make_async_copy(src, dst, load_sem.at[k])
+        for k, (src, dst) in enumerate(
+            (
+                (img_hbm.at[0], img),
+                (cw_hbm, cw),
+                (cot_hbm.at[0], cot),
+                (dw_hbm, dw),
+                (cb_hbm, cb),
+                (gain_hbm, gain_ref),
+                (shift_hbm, shift_ref),
+                (db_hbm, db),
+            )
+        )
+    ]
+    for load in loads:
+        load.start()
+
+    x_at, y_at = lax.div(r, 4), lax.rem(slot, 2)
+    hops = sorted(
+        ((min(dx, 4 - dx) + dy, dc, dx, dy) for dx in range(4) for dy in range(2) for dc in range(2)),
+        reverse=True,
+    )
+    row_peers = [
+        lax.rem(x_at + dx, 4) * 4
+        + (y_at if dy == 0 else 1 - y_at) * 2
+        + (core if dc == 0 else 1 - core)
+        for _, dc, dx, dy in hops[:-1]
+    ]
+    if dp_n == 32:
+        z_at, h_at = lax.div(d, 4), lax.rem(d, 4)
+        hops = sorted(
+            ((min(dz, 8 - dz) + 2 * min(dh, 4 - dh), dz, dh) for dz in range(8) for dh in range(4)),
+            reverse=True,
+        )
+        dp_peers = [
+            lax.rem(z_at + dz, 8) * 4 + lax.rem(h_at + dh, 4) for _, dz, dh in hops[:-1]
+        ]
+    else:
+        dp_peers = [lax.rem(d + i, dp_n) for i in range(1, dp_n)]
+
     barrier = pltpu.get_barrier_semaphore()
-
-    def greet_row(i, c):
-        pl.semaphore_signal(
-            barrier, inc=1, device_id={"rows": lax.rem(r + i, rows_n)}, device_id_type=MESH
-        )
-        return c
-
-    def greet_dp(i, c):
-        pl.semaphore_signal(
-            barrier, inc=1, device_id={"dp": lax.rem(d + i, dp_n)}, device_id_type=MESH
-        )
-        return c
-
-    lax.fori_loop(1, rows_n, greet_row, 0)
-    lax.fori_loop(1, dp_n, greet_dp, 0)
-
+    for to in dp_peers:
+        pl.semaphore_signal(barrier, inc=1, device_id={"dp": to}, device_id_type=MESH)
+    for to in row_peers:
+        pl.semaphore_signal(barrier, inc=1, device_id={"rows": to}, device_id_type=MESH)
+
+    pl.semaphore_wait(barrier, rows_n + dp_n - 2)
+    up = lax.max(r - 1, 0)
+    down = lax.min(r + 1, last)
+    mid = pl.ds(CHANS, 2 * CHANS)
+    img_down = remote(img_hbm.at[0, 1], edge_img.at[0], img_s.at[0], img_r.at[0], rows=down)
+    img_up = remote(img_hbm.at[0, 0], edge_img.at[1], img_s.at[1], img_r.at[1], rows=up)
+    cot_up = remote(cot_hbm.at[0], edge_cot, cot_s, cot_r, rows=up)
+    mix_down = remote(m4.at[2, :, mid], m4.at[0, :, mid], mix_s, mix_r, rows=down)
+    g_down = remote(g4.at[2, :, mid], g4.at[0, :, mid], g_s.at[0], g_r.at[0], rows=down)
+    g_up = remote(g4.at[1, :, mid], g4.at[3, :, mid], g_s.at[1], g_r.at[1], rows=up)
+
+    @pl.when(r < last)
+    def _():
+        img_down.start()
+
+    @pl.when(r > 0)
+    def _():
+        img_up.start()
+
+    loads[1].wait()
     zero_block = jnp.zeros((CHANS, CHANS), BF)
     for kh in range(3):
         for kw in range(3):
@@ -178,28 +249,10 @@
         edge_cot[...] = jnp.zeros(edge_cot.shape, BF)
         g4[3] = jnp.zeros(g4.shape[1:], BF)
 
-    pl.semaphore_wait(barrier, rows_n + dp_n - 2)
-    up = lax.max(r - 1, 0)
-    down = lax.min(r + 1, last)
-    img_down = remote(img.at[0, 1], edge_img.at[0], img_s.at[0], img_r.at[0], rows=down)
-    img_up = remote(img.at[0, 0], edge_img.at[1], img_s.at[1], img_r.at[1], rows=up)
-    cot_up = remote(cot.at[0], edge_cot, cot_s, cot_r, rows=up)
-    mix_down = remote(m4.at[2], m4.at[0], mix_s, mix_r, rows=down)
-    mid = pl.ds(CHANS, 2 * CHANS)
-    g_down = remote(g4.at[2, :, mid], g4.at[0, :, mid], g_s.at[0], g_r.at[0], rows=down)
-    g_up = remote(g4.at[1, :, mid], g4.at[3, :, mid], g_s.at[1], g_r.at[1], rows=up)
-
-    @pl.when(r < last)
-    def _():
-        img_down.start()
-
-    @pl.when(r > 0)
-    def _():
-        img_up.start()
-        cot_up.start()
-
+    for k in (0, 2, 3, 4, 5, 6, 7):
+        loads[k].wait()
     for a in range(2):
-        split_columns(img[0, a], a + 1)
+        split_columns(img[a], a + 1)
 
     bias = twice(cb[...])
     hid[0] = nn(x4[1], wf[1]) + nn(x4[2], wf[2]) + bias
@@ -216,24 +269,20 @@
     def _():
         img_up.wait_recv()
 
+    @pl.when(r > 0)
+    def _():
+        cot_up.start()
+
     split_columns(edge_img[1], 3)
     hid[1] += nn(x4[3], wf[2])
 
     def spread(table, send, recv):
-        def go(i, c):
-            to = lax.rem(r + i, rows_n)
+        for to in row_peers:
             remote(table.at[r], table.at[r], send.at[to], recv.at[r], rows=to).start()
-            return c
-
-        lax.fori_loop(1, rows_n, go, 0)
 
     def gathered(table, send, recv):
-        def go(i, c):
-            other = lax.rem(r + i, rows_n)
+        for other in row_peers:
             remote(table.at[other], table.at[other], send.at[other], recv.at[other], rows=other).wait()
-            return c
-
-        lax.fori_loop(1, rows_n, go, 0)
 
     def colsum(x):
         return jnp.sum(x, axis=0, keepdims=True)
@@ -256,7 +305,7 @@
         both = dw[kh, 1:3].reshape(2 * CHANS, OUTS)
         return nt(grad, both), nt(lead, dw[kh, 0])
 
-    own_cot = cot[0]
+    own_cot = cot[...]
     own_cot32 = own_cot.astype(F32)
     cot_sum = colsum(own_cot32)
     lead_cot = shifted(own_cot32, 1).astype(BF)
@@ -292,12 +341,6 @@
         mixed = (x4[a + 1, :, CHANS : 3 * CHANS].astype(F32) + pre * sig).astype(BF)
         m4[a + 1, :, CHANS:] = mixed
         m4[a + 1, :, :CHANS] = shifted(mixed[:, CHANS:].astype(F32), -1).astype(BF)
-        if a == 1:
-
-            @pl.when(r < last)
-            def _():
-                mix_down.start()
-
         gp = gmix[a] * sig * (1.0 + pre * (1.0 - sig))
         hid[a] = normed
         gpre[a] = gp
@@ -311,11 +354,27 @@
     stat_b[r, 4:8, :] = jnp.zeros((4, CHANS), F32)
     spread(stat_b, sb_s, sb_r)
 
+    @pl.when(r < last)
+    def _():
+        mix_down.start()
+
+    sub = lax.broadcasted_iota(jnp.int32, (CHANS, CHANS), 0) % 8
+
     def down_grad(kh):
         part = tn(own_cot, m4[kh])
         for kw in range(3):
-            c = 3 * kh + kw
-            full[c % 2, c // 2] = part[:, kw * CHANS : (kw + 1) * CHANS]
+            tap = 3 * kh + kw
+            tiles = part[:, kw * CHANS : (kw + 1) * CHANS].reshape(16, 2, 8, CHANS)
+            one = tiles[:, 0].reshape(CHANS, CHANS)
+            two = tiles[:, 1].reshape(CHANS, CHANS)
+            low = jnp.where(sub < 4, one, pltpu.roll(two, 4, 0))
+            high = jnp.where(sub < 4, pltpu.roll(one, CHANS - 4, 0), two)
+            if tap < 8:
+                early[0, tap] = low
+                early[1, tap] = high
+            else:
+                late[1, 4] = low
+                late[0, 5] = high
 
     def taps(kh):
         return dw[kh].reshape(3 * CHANS, OUTS)
@@ -327,13 +386,16 @@
     @pl.when(r > 0)
     def _():
         mix_down.wait_recv()
+        m4[0, :, :CHANS] = shifted(m4[0, :, 2 * CHANS :].astype(F32), -1).astype(BF)
 
     down_grad(0)
-    cs[0:4] = full[1 - core, 0:4].astype(BF)
-    pair_one = remote(cs.at[0:4], cr.at[0:4], c_s.at[0], c_r.at[0], rows=mate)
-    pair_two = remote(cs.at[4:PAIRS], cr.at[4:PAIRS], c_s.at[1], c_r.at[1], rows=mate)
+    cs[...] = early[1 - core].astype(BF)
+    pair_one = remote(cs, cr, c_s.at[0], c_r.at[0], rows=mate)
+    pair_two = remote(cs2, cr2, c_s.at[1], c_r.at[1], rows=mate)
     pair_one.start()
-    block_out[0, 0] = (out + nn(m4[0], taps(0))).astype(BF)
+    block_v[...] = (out + nn(m4[0], taps(0))).astype(BF)
+    block_store = pltpu.make_async_copy(block_v, block_out.at[0, 0], store_sem.at[0])
+    block_store.start()
 
     gathered(stat_b, sb_s, sb_r)
     totals = jnp.sum(stat_b[...], axis=0)
@@ -348,66 +410,49 @@
         grad = (rstd2 * (gpre[a] * gain2 - m1w - hid[a] * m2w)).astype(BF)
         g4[a + 1, :, CHANS : 3 * CHANS] = grad
 
-    @pl.when(r < last)
-    def _():
-        g_down.start()
-
-    @pl.when(r > 0)
-    def _():
-        g_up.start()
-
     n_channel = float(2 * cols * rows_n)
     tot_normed = (channel_sum - n_channel * mean) * rstd
     tot_bias = rstd * (gain_ref[...] * tot_gp - n_channel * m1 - m2 * tot_normed)
-    mine[0:1, :] = tot_bias
-    mine[1:2, :] = tot_gpn
-    mine[2:3, :] = tot_gp
-    mine[3:4, :] = totals[2:3]
-    mine[4:5, :] = totals[3:4]
-    mine[5:8, :] = jnp.zeros((3, CHANS), F32)
-
-    def row_send(low, high):
-        for i in range(1, slots):
-            to = lax.rem(slot + i, slots)
-
-            @pl.when((to >= low) & (to < high))
-            def _():
-                remote(
-                    rs.at[lax.min(to, PAIRS - 1)],
-                    rr.at[slot],
-                    r_s.at[to],
-                    r_r.at[slot],
-                    rows=2 * to + core,
-                ).start()
-
-    def pair_sum(low, high):
-        for k in range(low, high):
-            both = full[core, k] + cr[k].astype(F32)
-            full[core, k] = both
-            rs[k] = both.astype(BF)
-        row_send(low, high)
+    mine[...] = jnp.zeros(mine.shape, F32)
+    for k in (0, 4):
+        mine[0, k : k + 1, :] = tot_bias
+        mine[0, k + 1 : k + 2, :] = tot_gpn
+        mine[0, k + 2 : k + 3, :] = tot_gp
+        mine[1, k : k + 1, :] = totals[2:3]
+        mine[1, k + 1 : k + 2, :] = totals[3:4]
+
+    slot_peers = [
+        lax.rem(x_at + dx, 4) * 2 + (y_at if dy == 0 else 1 - y_at)
+        for dx, dy in ((2, 1), (2, 0), (1, 1), (3, 1), (1, 0), (3, 0), (0, 1))
+    ]
+
+    def early_send(to):
+        return remote(rs.at[to], rr.at[slot], r_s.at[to], r_r.at[slot], rows=2 * to + core)
+
+    def late_send(to):
+        return remote(
+            rs2.at[lax.min(to, LATE - 1)], rr2.at[slot], q_s.at[to], q_r.at[slot], rows=2 * to + core
+        )
 
     pair_one.wait()
-    pair_sum(0, 4)
-
-    sub = lax.broadcasted_iota(jnp.int32, (CHANS, CHANS), 0) % 8
-    conv_taps = []
+    both = early[core] + cr[...].astype(F32)
+    early[core] = both
+    rs[...] = both.astype(BF)
+    for to in slot_peers:
+        early_send(to).start()
+
     for kh in range(3):
         part = tn(g4[1, :, CHANS : 3 * CHANS], x4[kh]) + tn(
             g4[2, :, CHANS : 3 * CHANS], x4[kh + 1]
         )
         for kw in range(3):
-            conv_taps.append(
+            tap = 3 * kh + kw
+            late[tap % 2, tap // 2] = (
                 part[:CHANS, kw * CHANS : (kw + 1) * CHANS]
                 + part[CHANS:, (kw + 1) * CHANS : (kw + 2) * CHANS]
             )
-    conv_taps.append(jnp.zeros((CHANS, CHANS), F32))
-    for k in range(5):
-        c = DOWN_CHUNKS + k
-        one, two = conv_taps[2 * k], conv_taps[2 * k + 1]
-        full[c % 2, c // 2, :CHANS] = jnp.where(sub < 4, one, pltpu.roll(two, 4, 0))
-        full[c % 2, c // 2, CHANS:] = jnp.where(sub < 4, pltpu.roll(one, CHANS - 4, 0), two)
-    cs[4:PAIRS] = full[1 - core, 4:PAIRS].astype(BF)
+    late[1, 5] = jnp.zeros((CHANS, CHANS), F32)
+    cs2[...] = late[1 - core].astype(BF)
     pair_two.start()
 
     def sides(f):
@@ -415,18 +460,64 @@
         g4[f, :, :CHANS] = shifted(grad[:, CHANS:], -1).astype(BF)
         g4[f, :, 3 * CHANS :] = shifted(grad[:, :CHANS], 1).astype(BF)
 
+    pair_two.wait()
+    both = late[core] + cr2[...].astype(F32)
+    late[core] = both
+    rs2[...] = both.astype(BF)
+    for to in slot_peers:
+
+        @pl.when(to < LATE)
+        def _():
+            late_send(to).start()
+
+    @pl.when(r < last)
+    def _():
+        g_down.start()
+
+    @pl.when(r > 0)
+    def _():
+        g_up.start()
+
     sides(1)
     sides(2)
     gmix[0] += nt(g4[1], wb[1]) + nt(g4[2], wb[0])
     gmix[1] += nt(g4[1], wb[2]) + nt(g4[2], wb[1])
 
-    pair_two.wait()
-    pair_sum(4, PAIRS)
+    total = early[core, slot]
+    for other in slot_peers:
+        remote(rs.at[0], rr.at[other], r_s.at[other], r_r.at[other], rows=2 * other + core).wait_recv()
+        total = total + rr[other].astype(F32)
+    red1[...] = total
+
+    @pl.when(slot < LATE)
+    def _():
+        for other in slot_peers:
+            remote(rs2.at[0], rr2.at[other], q_s.at[other], q_r.at[other], rows=2 * other + core).wait_recv()
+        total = late[core, lax.min(slot, LATE - 1)]
+        for other in slot_peers:
+            total = total + rr2[other].astype(F32)
+        red2[...] = total
+
+    @pl.when(slot >= LATE)
+    def _():
+        red2[...] = jnp.broadcast_to(mine[core][None], (16, 8, CHANS)).reshape(CHANS, CHANS)
+
+    one, two = red1[...], red2[...]
+    red[:CHANS] = jnp.where(sub < 4, one, pltpu.roll(two, 4, 0))
+    red[CHANS:] = jnp.where(sub < 4, pltpu.roll(one, CHANS - 4, 0), two)
+
+    def place(e):
+        row = lax.rem(e, 2) * 16 + lax.div(e, 2)
+        return pl.ds(pl.multiple_of(row * 8, 8), 8)
+
+    for to in dp_peers:
+        remote(red.at[place(to)], dr.at[d], d_s.at[to], d_r.at[d], dp=to).start()
+    dr[d] = red[place(d), :]
 
     def put_row(a):
         tall[pl.ds(8, half, stride=2), :] = gmix[a, :, :CHANS]
         tall[pl.ds(9, half, stride=2), :] = gmix[a, :, CHANS:]
-        gimg_out[0, a] = tall[8 : cols + 8, :].astype(BF)
+        gimg_v[a] = tall[8 : cols + 8, :].astype(BF)
 
     @pl.when(r > 0)
     def _():
@@ -443,40 +534,11 @@
 
     gmix[1] += nt(g4[3], wb[0])
     put_row(1)
-
-    @pl.when(slot < PAIRS)
-    def _():
-        def take(i, total):
-            other = lax.rem(slot + i, slots)
-            remote(
-                rs.at[0], rr.at[other], r_s.at[other], r_r.at[other], rows=2 * other + core
-            ).wait_recv()
-            return total + rr[other].astype(F32)
-
-        red[...] = lax.fori_loop(1, slots, take, full[core, lax.min(slot, PAIRS - 1)])
-
-    @pl.when(slot == PAIRS)
-    def _():
-        red[...] = jnp.broadcast_to(mine[...][None], (32, 8, CHANS)).reshape(256, CHANS)
-
-    def place(e):
-        row = jnp.where(r < DOWN_CHUNKS, e, lax.rem(e, 2) * 16 + lax.div(e, 2))
-        return pl.ds(pl.multiple_of(row * 8, 8), 8)
-
-    def to_owner(i, c):
-        to = lax.rem(d + i, dp_n)
-        remote(red.at[place(to)], dr.at[d], d_s.at[to], d_r.at[d], dp=to).start()
-        return c
-
-    lax.fori_loop(1, dp_n, to_owner, 0)
-    dr[d] = red[place(d), :]
-
-    def from_peer(i, c):
-        other = lax.rem(d + i, dp_n)
+    gimg_store = pltpu.make_async_copy(gimg_v, gimg_out.at[0], store_sem.at[1])
+    gimg_store.start()
+
+    for other in dp_peers:
         remote(red.at[place(other)], dr.at[other], d_s.at[other], d_r.at[other], dp=other).wait()
-        return c
-
-    lax.fori_loop(1, dp_n, from_peer, 0)
     gout[r] = jnp.sum(dr[...], axis=0)
     spread(gout, o_s, o_r)
     gathered(gout, o_s, o_r)
@@ -493,12 +555,56 @@
         cot_up.wait_send()
         g_up.wait_send()
 
-    for i in range(1, slots):
-        to = lax.rem(slot + i, slots)
-
-        @pl.when(to < PAIRS)
+    for to in slot_peers:
+        early_send(to).wait_send()
+
+        @pl.when(to < LATE)
         def _():
-            remote(rs.at[0], rr.at[slot], r_s.at[to], r_r.at[slot], rows=2 * to + core).wait_send()
+            late_send(to).wait_send()
+
+    block_store.wait()
+    gimg_store.wait()
+
+
+def finish(
+    block, gimg, table, block_out, gimg_out, conv_out, bias_out, gain_out, shift_out, down_out, db_out,
+    conv_v, down_v, bias_v, gain_v, shift_v, db_v, sems,
+):
+    copies = [
+        pltpu.make_async_copy(src, dst, sems.at[k])
+        for k, (src, dst) in enumerate(
+            (
+                (block, block_out),
+                (gimg, gimg_out),
+                (conv_v, conv_out),
+                (down_v, down_out),
+                (bias_v, bias_out),
+                (gain_v, gain_out),
+                (shift_v, shift_out),
+                (db_v, db_out),
+            )
+        )
+    ]
+    copies[0].start()
+    copies[1].start()
+    for tap in range(TAPS):
+        conv_v[tap] = table[tap, 4:8]
+        if tap < 8:
+            down_v[tap, 0:4] = table[2 * tap, 0:4]
+            down_v[tap, 4:8] = table[2 * tap + 1, 0:4]
+    down_v[8, 0:4] = table[9, 4:8]
+    down_v[8, 4:8] = table[10, 4:8]
+    d = lax.axis_index("dp")
+    narrow = pltpu.roll(table[12], lax.rem(CHANS - 4 * d, CHANS), 1)
+    bias_v[...] = narrow[4:5, :4]
+    gain_v[...] = narrow[5:6, :4]
+    shift_v[...] = narrow[6:7, :4]
+    wide = pltpu.roll(table[13], lax.rem(2 * CHANS - 8 * d, CHANS), 1)
+    db_v[...] = jnp.where(d < 16, wide[4:5, :8], wide[5:6, :8])
+    for copy in copies[2:]:
+        copy.start()
+    for copy in copies:
+        copy.wait()
 
 
 def shards(
@@ -510,7 +616,20 @@
     half = cols // 2
     vmem = pl.BlockSpec(memory_space=pltpu.VMEM)
     dma = pltpu.SemaphoreType.DMA
+    anywhere = pl.BlockSpec(memory_space=pl.ANY)
+    unit = (CHANS, CHANS)
+    slots = rows_n // 2
     scratch = [
+        pltpu.VMEM((local_rows, cols, chans), BF),
+        pltpu.VMEM(conv_weight.shape, BF),
+        pltpu.VMEM((1, CHANS), F32),
+        pltpu.VMEM((1, CHANS), F32),
+        pltpu.VMEM((1, CHANS), F32),
+        pltpu.VMEM(down_weight.shape, BF),
+        pltpu.VMEM((1, OUTS), F32),
+        pltpu.VMEM((half, OUTS), BF),
+        pltpu.VMEM((half, OUTS), BF),
+        pltpu.VMEM((local_rows, cols, chans), BF),
         pltpu.VMEM((half + 16, OUTS), F32),
         pltpu.VMEM((cols + 16, CHANS), F32),
         pltpu.VMEM((2, cols, CHANS), BF),
@@ -525,14 +644,23 @@
         pltpu.VMEM((2, half, 2 * CHANS), F32),
         pltpu.VMEM((rows_n, 8, CHANS), F32),
         pltpu.VMEM((rows_n, 8, CHANS), F32),
-        pltpu.VMEM((8, CHANS), F32),
-        pltpu.VMEM((2, PAIRS, OUTS, CHANS), F32),
-        pltpu.VMEM((PAIRS, OUTS, CHANS), BF),
-        pltpu.VMEM((PAIRS, OUTS, CHANS), BF),
-        pltpu.VMEM((PAIRS, OUTS, CHANS), BF),
-        pltpu.VMEM((rows_n // 2, OUTS, CHANS), BF),
+        pltpu.VMEM((2, 8, CHANS), F32),
+        pltpu.VMEM((2, slots) + unit, F32),
+        pltpu.VMEM((2, LATE) + unit, F32),
+        pltpu.VMEM((slots,) + unit, BF),
+        pltpu.VMEM((slots,) + unit, BF),
+        pltpu.VMEM((LATE,) + unit, BF),
+        pltpu.VMEM((LATE,) + unit, BF),
+        pltpu.VMEM((slots,) + unit, BF),
+        pltpu.VMEM((slots,) + unit, BF),
+        pltpu.VMEM((LATE,) + unit, BF),
+        pltpu.VMEM((slots,) + unit, BF),
+        pltpu.VMEM(unit, F32),
+        pltpu.VMEM(unit, F32),
         pltpu.VMEM((OUTS, CHANS), F32),
         pltpu.VMEM((dp_n, 8, CHANS), F32),
+        dma((8,)),
+        dma((2,)),
         dma((2,)),
         dma((2,)),
         dma,
@@ -547,8 +675,10 @@
         dma((rows_n,)),
         dma((2,)),
         dma((2,)),
-        dma((rows_n // 2,)),
-        dma((rows_n // 2,)),
+        dma((slots,)),
+        dma((slots,)),
+        dma((slots,)),
+        dma((slots,)),
         dma((dp_n,)),
         dma((dp_n,)),
         dma((rows_n,)),
@@ -565,11 +695,11 @@
             jax.ShapeDtypeStruct((1, local_rows, cols, chans), BF),
             jax.ShapeDtypeStruct((rows_n, 8, CHANS), F32),
         ),
-        in_specs=[vmem] * 8,
-        out_specs=(vmem, vmem, vmem),
+        in_specs=[anywhere] * 8,
+        out_specs=(anywhere, anywhere, vmem),
         scratch_shapes=scratch,
         compiler_params=pltpu.CompilerParams(
-            collective_id=0, has_side_effects=True, vmem_limit_bytes=40 * 1024 * 1024
+            collective_id=0, has_side_effects=True, vmem_limit_bytes=56 * 1024 * 1024
         ),
         name="step",
     )(
@@ -582,15 +712,43 @@
         down_bias.reshape(1, OUTS),
         cotangent.reshape(1, half, OUTS),
     )
-    d = lax.axis_index("dp")
-    down_part = jnp.swapaxes(table[:DOWN_CHUNKS], 1, 2).reshape(3, 3, CHANS, 8)
-    conv_part = jnp.swapaxes(
-        table[DOWN_CHUNKS:14].reshape(10, 4, CHANS)[:9], 1, 2
-    ).reshape(3, 3, CHANS, 4)
-    vectors = table[14]
-    narrow = lax.dynamic_slice(vectors, (0, 4 * d), (3, 4))
-    wide = lax.dynamic_slice(vectors[3:5].reshape(OUTS), (8 * d,), (8,))
-    return block, grad_image, conv_part, narrow[0], narrow[1], narrow[2], down_part, wide
+    shape = jax.ShapeDtypeStruct
+    outs = pl.pallas_call(
+        finish,
+        out_shape=(
+            shape(block.shape, BF),
+            shape(grad_image.shape, BF),
+            shape((TAPS, 4, CHANS), F32),
+            shape((1, 4), F32),
+            shape((1, 4), F32),
+            shape((1, 4), F32),
+            shape((TAPS, 8, CHANS), F32),
+            shape((1, 8), F32),
+        ),
+        in_specs=[anywhere, anywhere, vmem],
+        out_specs=[anywhere] * 8,
+        scratch_shapes=[
+            pltpu.VMEM((TAPS, 4, CHANS), F32),
+            pltpu.VMEM((TAPS, 8, CHANS), F32),
+            pltpu.VMEM((1, 4), F32),
+            pltpu.VMEM((1, 4), F32),
+            pltpu.VMEM((1, 4), F32),
+            pltpu.VMEM((1, 8), F32),
+            dma((8,)),
+        ],
+        name="finish",
+    )(block, grad_image, table)
+    block, grad_image, conv_t, bias, gain, shift, down_t, down_bias_grad = outs
+    return (
+        block,
+        grad_image,
+        jnp.swapaxes(conv_t, 1, 2).reshape(3, 3, CHANS, 4),
+        bias.reshape(4),
+        gain.reshape(4),
+        shift.reshape(4),
+        jnp.swapaxes(down_t, 1, 2).reshape(3, 3, CHANS, 8),
+        down_bias_grad.reshape(8),
+    )
 
 
 def solution(mesh):

time: 66.1 us -> 69 us (1.044)
  Pallas kernels: 56.8 us -> 68.2 us
  local copies, waits for them, and re-layouts: 8.34 us -> 0 us
    pallas_call x0 -> x1, Pallas kernels: none -> 13.9 us  [shards(): pl.pallas_call(finish, out_shape=(shape(block.shape, BF), shape(grad_imag...]
    unnamed x18 -> x0, local copies, waits for them, and re-layouts: 5.92 us -> none
    pallas_call x1, Pallas kernels: 56.8 us -> 54.3 us  [shards(): pl.pallas_call(body, out_shape=(jax.ShapeDtypeStruct((1, 1, half, OUTS),...]
    slice x4 -> x0, local copies, waits for them, and re-layouts: 1.23 us -> none  [the longest x1 0.62 us: shards(): down_part = jnp.swapaxes(table[:DOWN_CHUNKS], 1, 2).reshape(3, 3, CHANS, 8)]
where the time goes in v2:
time: 69 us; the launch traced here: 68.9 us
  Pallas kernels  68.2 us (99%)
    pallas_call x1, Pallas kernels, shards(): pl.pallas_call(body, out_shape=(jax.ShapeDtypeStruct((1, 1, half, OUTS),...  54.3 us
    pallas_call x1, Pallas kernels, shards(): pl.pallas_call(finish, out_shape=(shape(block.shape, BF), shape(grad_imag...  13.9 us

profile of v2, /device:TPU:1, one launch (start us, length us, event | category | flops | bytes accessed | tf_op | source)
XLA Modules:
  0.0 68.9 jit_solution(9610978246396586229)
XLA Ops:
  0.6 54.3 %step.1 = (bf16[1,1,256,256]{3,2,1,0:T(8,128)(2,1)}, bf16[1,2,512,128]{3,2,1,0:T(8,128)(2,1)}, f32[16,8,128]{2,1,0:T(8,128)}) custom-call(bf16[1,2,512,128]{3,2,1,0:T(8,128)(2,1)} %refs_0_.1, bf16[3,3,128,128]{3,2,1,0:T(8,128)(2,1)} %refs_1_.1, f32[1,128]{1,0:T(1,128)} %bitcast.17, f32[1,128]{1,0:T(1,128)} %bitcast.18, f32[1,128]{1,0:T(1,128)} %bitcast.19, ...), custom_call_target="tpu_custom_call" | custom-call | tf_op jit(solution)/shard_map/step/pallas_call | solution.py:691
  54.9 13.9 %finish.1 = (bf16[1,1,256,256]{3,2,1,0:T(8,128)(2,1)}, bf16[1,2,512,128]{3,2,1,0:T(8,128)(2,1)}, f32[9,4,128]{2,1,0:T(4,128)}, f32[1,4]{1,0:T(1,128)}, f32[1,4]{...) custom-call(bf16[1,1,256,256]{3,2,1,0:T(8,128)(2,1)} %get-tuple-element.19.block, ...), custom_call_target="tpu_custom_call" | custom-call | tf_op jit(solution)/shard_map/finish/pallas_call | solution.py:716

commit v3 on v2

--- a/solution.py
+++ b/solution.py
@@ -64,8 +64,6 @@
     dw,
     db,
     cot,
-    block_v,
-    gimg_v,
     wide,
     tall,
     edge_img,
@@ -96,7 +94,6 @@
     red,
     dr,
     load_sem,
-    store_sem,
     img_s,
     img_r,
     cot_s,
@@ -393,9 +390,7 @@
     pair_one = remote(cs, cr, c_s.at[0], c_r.at[0], rows=mate)
     pair_two = remote(cs2, cr2, c_s.at[1], c_r.at[1], rows=mate)
     pair_one.start()
-    block_v[...] = (out + nn(m4[0], taps(0))).astype(BF)
-    block_store = pltpu.make_async_copy(block_v, block_out.at[0, 0], store_sem.at[0])
-    block_store.start()
+    block_out[0, 0] = (out + nn(m4[0], taps(0))).astype(BF)
 
     gathered(stat_b, sb_s, sb_r)
     totals = jnp.sum(stat_b[...], axis=0)
@@ -517,7 +512,7 @@
     def put_row(a):
         tall[pl.ds(8, half, stride=2), :] = gmix[a, :, :CHANS]
         tall[pl.ds(9, half, stride=2), :] = gmix[a, :, CHANS:]
-        gimg_v[a] = tall[8 : cols + 8, :].astype(BF)
+        gimg_out[0, a] = tall[8 : cols + 8, :].astype(BF)
 
     @pl.when(r > 0)
     def _():
@@ -534,8 +529,6 @@
 
     gmix[1] += nt(g4[3], wb[0])
     put_row(1)
-    gimg_store = pltpu.make_async_copy(gimg_v, gimg_out.at[0], store_sem.at[1])
-    gimg_store.start()
 
     for other in dp_peers:
         remote(red.at[place(other)], dr.at[other], d_s.at[other], d_r.at[other], dp=other).wait()
@@ -561,9 +554,6 @@
         @pl.when(to < LATE)
         def _():
             late_send(to).wait_send()
-
-    block_store.wait()
-    gimg_store.wait()
 
 
 def finish(
@@ -616,7 +606,7 @@
     half = cols // 2
     vmem = pl.BlockSpec(memory_space=pltpu.VMEM)
     dma = pltpu.SemaphoreType.DMA
-    anywhere = pl.BlockSpec(memory_space=pl.ANY)
+    anywhere = pl.BlockSpec(memory_space=pltpu.HBM)
     unit = (CHANS, CHANS)
     slots = rows_n // 2
     scratch = [
@@ -628,8 +618,6 @@
         pltpu.VMEM(down_weight.shape, BF),
         pltpu.VMEM((1, OUTS), F32),
         pltpu.VMEM((half, OUTS), BF),
-        pltpu.VMEM((half, OUTS), BF),
-        pltpu.VMEM((local_rows, cols, chans), BF),
         pltpu.VMEM((half + 16, OUTS), F32),
         pltpu.VMEM((cols + 16, CHANS), F32),
         pltpu.VMEM((2, cols, CHANS), BF),
@@ -662,7 +650,6 @@
         dma((8,)),
         dma((2,)),
         dma((2,)),
-        dma((2,)),
         dma,
         dma,
         dma,
@@ -696,13 +683,13 @@
             jax.ShapeDtypeStruct((rows_n, 8, CHANS), F32),
         ),
         in_specs=[anywhere] * 8,
-        out_specs=(anywhere, anywhere, vmem),
+        out_specs=(vmem, vmem, vmem),
         scratch_shapes=scratch,
         compiler_params=pltpu.CompilerParams(
-            collective_id=0, has_side_effects=True, vmem_limit_bytes=56 * 1024 * 1024
+            collective_id=0, has_side_effects=True, vmem_limit_bytes=40 * 1024 * 1024
         ),
         name="step",
-    )(
+    )(*(pltpu.with_memory_space_constraint(x, pltpu.HBM) for x in (
         images,
         conv_weight,
         conv_bias.reshape(1, CHANS),
@@ -711,7 +698,7 @@
         down_weight,
         down_bias.reshape(1, OUTS),
         cotangent.reshape(1, half, OUTS),
-    )
+    )))
     shape = jax.ShapeDtypeStruct
     outs = pl.pallas_call(
         finish,
@@ -725,7 +712,7 @@
             shape((TAPS, 8, CHANS), F32),
             shape((1, 8), F32),
         ),
-        in_specs=[anywhere, anywhere, vmem],
+        in_specs=[vmem, vmem, vmem],
         out_specs=[anywhere] * 8,
         scratch_shapes=[
             pltpu.VMEM((TAPS, 4, CHANS), F32),
@@ -736,6 +723,7 @@
             pltpu.VMEM((1, 8), F32),
             dma((8,)),
         ],
+        compiler_params=pltpu.CompilerParams(vmem_limit_bytes=4 * 1024 * 1024),
         name="finish",
     )(block, grad_image, table)
     block, grad_image, conv_t, bias, gain, shift, down_t, down_bias_grad = outs

time: 69 us -> 55.3 us (0.80)
  Pallas kernels: 68.2 us -> 54.5 us
    pallas_call x1, Pallas kernels: 13.9 us -> 0.84 us  [shards(): pl.pallas_call(finish, out_shape=(shape(block.shape, BF), shape(grad_imag...]
where the time goes in v3:
time: 55.3 us; the launch traced here: 55.1 us
  Pallas kernels  54.5 us (99%)
  between operations  0.64 us (1%)
    pallas_call x1, Pallas kernels, shards(): pl.pallas_call(body, out_shape=(jax.ShapeDtypeStruct((1, 1, half, OUTS),...  53.7 us

profile of v3, /device:TPU:1, one launch (start us, length us, event | category | flops | bytes accessed | tf_op | source)
XLA Modules:
  0.0 55.1 jit_solution(8915710878379293709)
XLA Ops:
  0.6 53.7 %step.1 = (bf16[1,1,256,256]{3,2,1,0:T(8,128)(2,1)S(1)}, bf16[1,2,512,128]{3,2,1,0:T(8,128)(2,1)S(1)}, f32[16,8,128]{2,1,0:T(8,128)S(1)}) custom-call(bf16[1,2,512,128]{3,2,1,0:T(8,128)(2,1)} %refs_0_.1, bf16[3,3,128,128]{3,2,1,0:T(8,128)(2,1)} %refs_1_.1, f32[1,128]{1,0:T(1,128)} %bitcast.17, f32[1,128]{1,0:T(1,128)} %bitcast.18, f32[1,128]{1,0:T(1,128)} %bitcast.19, ...), custom_call_target="tpu_custom_call" | custom-call | tf_op jit(solution)/shard_map/step/pallas_call | solution.py:678
  54.3 0.8 %finish.1 = (bf16[1,1,256,256]{3,2,1,0:T(8,128)(2,1)}, bf16[1,2,512,128]{3,2,1,0:T(8,128)(2,1)}, f32[9,4,128]{2,1,0:T(4,128)}, f32[1,4]{1,0:T(1,128)}, f32[1,4]{...) custom-call(bf16[1,1,256,256]{3,2,1,0:T(8,128)(2,1)S(1)} %get-tuple-element.19.block, ...), custom_call_target="tpu_custom_call" | custom-call | tf_op jit(solution)/shard_map/finish/pallas_call | solution.py:703

commit v4 on v3

--- a/solution.py
+++ b/solution.py
@@ -13,7 +13,7 @@
 MESH = pl.DeviceIdType.MESH
 EPS = 1e-05
 TAPS = 9
-LATE = 6
+EARLY = 6
 
 
 def nn(a, b):
@@ -76,6 +76,7 @@
     hid,
     gpre,
     gmix,
+    hold,
     stat_a,
     stat_b,
     mine,
@@ -154,9 +155,6 @@
             )
         )
     ]
-    for load in loads:
-        load.start()
-
     x_at, y_at = lax.div(r, 4), lax.rem(slot, 2)
     hops = sorted(
         ((min(dx, 4 - dx) + dy, dc, dx, dy) for dx in range(4) for dy in range(2) for dc in range(2)),
@@ -186,6 +184,9 @@
     for to in row_peers:
         pl.semaphore_signal(barrier, inc=1, device_id={"rows": to}, device_id_type=MESH)
 
+    for load in loads:
+        load.start()
+
     pl.semaphore_wait(barrier, rows_n + dp_n - 2)
     up = lax.max(r - 1, 0)
     down = lax.min(r + 1, last)
@@ -204,6 +205,7 @@
     @pl.when(r > 0)
     def _():
         img_up.start()
+        cot_up.start()
 
     loads[1].wait()
     zero_block = jnp.zeros((CHANS, CHANS), BF)
@@ -266,20 +268,16 @@
     def _():
         img_up.wait_recv()
 
-    @pl.when(r > 0)
-    def _():
-        cot_up.start()
-
     split_columns(edge_img[1], 3)
     hid[1] += nn(x4[3], wf[2])
 
     def spread(table, send, recv):
         for to in row_peers:
-            remote(table.at[r], table.at[r], send.at[to], recv.at[r], rows=to).start()
-
-    def gathered(table, send, recv):
-        for other in row_peers:
-            remote(table.at[other], table.at[other], send.at[other], recv.at[other], rows=other).wait()
+            remote(table.at[r], table.at[r], send, recv, rows=to).start()
+
+    def whole(table, send, recv):
+        part = table.at[pl.ds(0, rows_n - 1)]
+        return remote(part, part, send, recv, rows=mate)
 
     def colsum(x):
         return jnp.sum(x, axis=0, keepdims=True)
@@ -306,18 +304,18 @@
     own_cot32 = own_cot.astype(F32)
     cot_sum = colsum(own_cot32)
     lead_cot = shifted(own_cot32, 1).astype(BF)
-    whole, odd = pull(own_cot, lead_cot, 1)
-    gmix[0] = whole
+    full, odd = pull(own_cot, lead_cot, 1)
+    gmix[0] = full
     gmix[0, :, CHANS:] += odd
-    whole, odd = pull(own_cot, lead_cot, 2)
-    gmix[1] = whole
+    full, odd = pull(own_cot, lead_cot, 2)
+    gmix[1] = full
     gmix[1, :, CHANS:] += odd
     below = edge_cot[...]
-    whole, odd = pull(below, shifted(below.astype(F32), 1).astype(BF), 0)
-    gmix[1] += whole
+    full, odd = pull(below, shifted(below.astype(F32), 1).astype(BF), 0)
+    gmix[1] += full
     gmix[1, :, CHANS:] += odd
 
-    gathered(stat_a, sa_s, sa_r)
+    whole(stat_a, sa_s, sa_r).wait_recv()
     table = stat_a[...]
     groups = group_sum(table.reshape(rows_n * 8, CHANS)).reshape(rows_n, 8, CHANS)
     group_tot = jnp.sum(groups, axis=0)
@@ -337,7 +335,6 @@
         sig = jax.nn.sigmoid(pre)
         mixed = (x4[a + 1, :, CHANS : 3 * CHANS].astype(F32) + pre * sig).astype(BF)
         m4[a + 1, :, CHANS:] = mixed
-        m4[a + 1, :, :CHANS] = shifted(mixed[:, CHANS:].astype(F32), -1).astype(BF)
         gp = gmix[a] * sig * (1.0 + pre * (1.0 - sig))
         hid[a] = normed
         gpre[a] = gp
@@ -366,33 +363,58 @@
             two = tiles[:, 1].reshape(CHANS, CHANS)
             low = jnp.where(sub < 4, one, pltpu.roll(two, 4, 0))
             high = jnp.where(sub < 4, pltpu.roll(one, CHANS - 4, 0), two)
-            if tap < 8:
-                early[0, tap] = low
-                early[1, tap] = high
+            if tap >= 3:
+                early[0, tap - 3] = low
+                early[1, tap - 3] = high
             else:
-                late[1, 4] = low
-                late[0, 5] = high
+                late[1, 4 + tap] = low
+                late[0, 5 + tap] = high
 
     def taps(kh):
         return dw[kh].reshape(3 * CHANS, OUTS)
 
-    out = nn(m4[1], taps(1)) + nn(m4[2], taps(2)) + db[...]
+    for a in range(2):
+        m4[a + 1, :, :CHANS] = shifted(m4[a + 1, :, 2 * CHANS :].astype(F32), -1).astype(BF)
+
     down_grad(1)
     down_grad(2)
-
-    @pl.when(r > 0)
-    def _():
-        mix_down.wait_recv()
-        m4[0, :, :CHANS] = shifted(m4[0, :, 2 * CHANS :].astype(F32), -1).astype(BF)
-
-    down_grad(0)
     cs[...] = early[1 - core].astype(BF)
     pair_one = remote(cs, cr, c_s.at[0], c_r.at[0], rows=mate)
     pair_two = remote(cs2, cr2, c_s.at[1], c_r.at[1], rows=mate)
     pair_one.start()
-    block_out[0, 0] = (out + nn(m4[0], taps(0))).astype(BF)
-
-    gathered(stat_b, sb_s, sb_r)
+    out = nn(m4[1], taps(1)) + nn(m4[2], taps(2)) + db[...]
+    hold[...] = out
+
+    slot_peers = [
+        lax.rem(x_at + dx, 4) * 2 + (y_at if dy == 0 else 1 - y_at)
+        for dx, dy in ((2, 1), (2, 0), (1, 1), (3, 1), (1, 0), (3, 0), (0, 1))
+    ]
+
+    def early_send(to):
+        return remote(rs.at[lax.min(to, EARLY - 1)], rr.at[slot], r_s.at[to], r_r, rows=2 * to + core)
+
+    def late_send(to):
+        return remote(rs2.at[to], rr2.at[slot], q_s.at[to], q_r, rows=2 * to + core)
+
+    pair_one.wait()
+    both = early[core] + cr[...].astype(F32)
+    early[core] = both
+    rs[...] = both.astype(BF)
+    for to in slot_peers:
+
+        @pl.when(to < EARLY)
+        def _():
+            early_send(to).start()
+
+    @pl.when(r > 0)
+    def _():
+        mix_down.wait_recv()
+        m4[0, :, :CHANS] = shifted(m4[0, :, 2 * CHANS :].astype(F32), -1).astype(BF)
+
+    down_grad(0)
+    block_out[0, 0] = (hold[...] + nn(m4[0], taps(0))).astype(BF)
+
+    whole(stat_b, sb_s, sb_r).wait_recv()
     totals = jnp.sum(stat_b[...], axis=0)
     tot_gp = totals[0:1]
     tot_gpn = totals[1:2]
@@ -416,26 +438,6 @@
         mine[1, k : k + 1, :] = totals[2:3]
         mine[1, k + 1 : k + 2, :] = totals[3:4]
 
-    slot_peers = [
-        lax.rem(x_at + dx, 4) * 2 + (y_at if dy == 0 else 1 - y_at)
-        for dx, dy in ((2, 1), (2, 0), (1, 1), (3, 1), (1, 0), (3, 0), (0, 1))
-    ]
-
-    def early_send(to):
-        return remote(rs.at[to], rr.at[slot], r_s.at[to], r_r.at[slot], rows=2 * to + core)
-
-    def late_send(to):
-        return remote(
-            rs2.at[lax.min(to, LATE - 1)], rr2.at[slot], q_s.at[to], q_r.at[slot], rows=2 * to + core
-        )
-
-    pair_one.wait()
-    both = early[core] + cr[...].astype(F32)
-    early[core] = both
-    rs[...] = both.astype(BF)
-    for to in slot_peers:
-        early_send(to).start()
-
     for kh in range(3):
         part = tn(g4[1, :, CHANS : 3 * CHANS], x4[kh]) + tn(
             g4[2, :, CHANS : 3 * CHANS], x4[kh + 1]
@@ -446,7 +448,7 @@
                 part[:CHANS, kw * CHANS : (kw + 1) * CHANS]
                 + part[CHANS:, (kw + 1) * CHANS : (kw + 2) * CHANS]
             )
-    late[1, 5] = jnp.zeros((CHANS, CHANS), F32)
+    late[1, 7] = jnp.zeros((CHANS, CHANS), F32)
     cs2[...] = late[1 - core].astype(BF)
     pair_two.start()
 
@@ -460,10 +462,7 @@
     late[core] = both
     rs2[...] = both.astype(BF)
     for to in slot_peers:
-
-        @pl.when(to < LATE)
-        def _():
-            late_send(to).start()
+        late_send(to).start()
 
     @pl.when(r < last)
     def _():
@@ -478,24 +477,25 @@
     gmix[0] += nt(g4[1], wb[1]) + nt(g4[2], wb[0])
     gmix[1] += nt(g4[1], wb[2]) + nt(g4[2], wb[1])
 
-    total = early[core, slot]
+    others = pl.ds(0, slots - 1)
+
+    @pl.when(slot < EARLY)
+    def _():
+        remote(rr.at[others], rr.at[others], r_s.at[slot], r_r, rows=mate).wait_recv()
+        total = early[core, lax.min(slot, EARLY - 1)]
+        for other in slot_peers:
+            total = total + rr[other].astype(F32)
+        red1[...] = total
+
+    @pl.when(slot >= EARLY)
+    def _():
+        red1[...] = jnp.broadcast_to(mine[core][None], (16, 8, CHANS)).reshape(CHANS, CHANS)
+
+    remote(rr2.at[others], rr2.at[others], q_s.at[slot], q_r, rows=mate).wait_recv()
+    total = late[core, slot]
     for other in slot_peers:
-        remote(rs.at[0], rr.at[other], r_s.at[other], r_r.at[other], rows=2 * other + core).wait_recv()
-        total = total + rr[other].astype(F32)
-    red1[...] = total
-
-    @pl.when(slot < LATE)
-    def _():
-        for other in slot_peers:
-            remote(rs2.at[0], rr2.at[other], q_s.at[other], q_r.at[other], rows=2 * other + core).wait_recv()
-        total = late[core, lax.min(slot, LATE - 1)]
-        for other in slot_peers:
-            total = total + rr2[other].astype(F32)
-        red2[...] = total
-
-    @pl.when(slot >= LATE)
-    def _():
-        red2[...] = jnp.broadcast_to(mine[core][None], (16, 8, CHANS)).reshape(CHANS, CHANS)
+        total = total + rr2[other].astype(F32)
+    red2[...] = total
 
     one, two = red1[...], red2[...]
     red[:CHANS] = jnp.where(sub < 4, one, pltpu.roll(two, 4, 0))
@@ -506,7 +506,7 @@
         return pl.ds(pl.multiple_of(row * 8, 8), 8)
 
     for to in dp_peers:
-        remote(red.at[place(to)], dr.at[d], d_s.at[to], d_r.at[d], dp=to).start()
+        remote(red.at[place(to)], dr.at[d], d_s, d_r, dp=to).start()
     dr[d] = red[place(d), :]
 
     def put_row(a):
@@ -530,11 +530,13 @@
     gmix[1] += nt(g4[3], wb[0])
     put_row(1)
 
-    for other in dp_peers:
-        remote(red.at[place(other)], dr.at[other], d_s.at[other], d_r.at[other], dp=other).wait()
+    if dp_n > 1:
+        part = dr.at[pl.ds(0, dp_n - 1)]
+        dp_round = remote(part, part, d_s, d_r, rows=mate)
+        dp_round.wait_recv()
     gout[r] = jnp.sum(dr[...], axis=0)
     spread(gout, o_s, o_r)
-    gathered(gout, o_s, o_r)
+    whole(gout, o_s, o_r).wait()
 
     @pl.when(r < last)
     def _():
@@ -548,12 +550,16 @@
         cot_up.wait_send()
         g_up.wait_send()
 
+    whole(stat_a, sa_s, sa_r).wait_send()
+    whole(stat_b, sb_s, sb_r).wait_send()
+    if dp_n > 1:
+        dp_round.wait_send()
     for to in slot_peers:
-        early_send(to).wait_send()
-
-        @pl.when(to < LATE)
+        late_send(to).wait_send()
+
+        @pl.when(to < EARLY)
         def _():
-            late_send(to).wait_send()
+            early_send(to).wait_send()
 
 
 def finish(
@@ -579,18 +585,19 @@
     copies[1].start()
     for tap in range(TAPS):
         conv_v[tap] = table[tap, 4:8]
-        if tap < 8:
-            down_v[tap, 0:4] = table[2 * tap, 0:4]
-            down_v[tap, 4:8] = table[2 * tap + 1, 0:4]
-    down_v[8, 0:4] = table[9, 4:8]
-    down_v[8, 4:8] = table[10, 4:8]
+        if tap < 3:
+            down_v[tap, 0:4] = table[9 + 2 * tap, 4:8]
+            down_v[tap, 4:8] = table[10 + 2 * tap, 4:8]
+        else:
+            down_v[tap, 0:4] = table[2 * tap - 6, 0:4]
+            down_v[tap, 4:8] = table[2 * tap - 5, 0:4]
     d = lax.axis_index("dp")
     narrow = pltpu.roll(table[12], lax.rem(CHANS - 4 * d, CHANS), 1)
-    bias_v[...] = narrow[4:5, :4]
-    gain_v[...] = narrow[5:6, :4]
-    shift_v[...] = narrow[6:7, :4]
+    bias_v[...] = narrow[0:1, :4]
+    gain_v[...] = narrow[1:2, :4]
+    shift_v[...] = narrow[2:3, :4]
     wide = pltpu.roll(table[13], lax.rem(2 * CHANS - 8 * d, CHANS), 1)
-    db_v[...] = jnp.where(d < 16, wide[4:5, :8], wide[5:6, :8])
+    db_v[...] = jnp.where(d < 16, wide[0:1, :8], wide[1:2, :8])
     for copy in copies[2:]:
         copy.start()
     for copy in copies:
@@ -630,18 +637,19 @@
         pltpu.VMEM((2, half, 2 * CHANS), F32),
         pltpu.VMEM((2, half, 2 * CHANS), F32),
         pltpu.VMEM((2, half, 2 * CHANS), F32),
+        pltpu.VMEM((half, OUTS), F32),
         pltpu.VMEM((rows_n, 8, CHANS), F32),
         pltpu.VMEM((rows_n, 8, CHANS), F32),
         pltpu.VMEM((2, 8, CHANS), F32),
+        pltpu.VMEM((2, EARLY) + unit, F32),
         pltpu.VMEM((2, slots) + unit, F32),
-        pltpu.VMEM((2, LATE) + unit, F32),
+        pltpu.VMEM((EARLY,) + unit, BF),
+        pltpu.VMEM((EARLY,) + unit, BF),
         pltpu.VMEM((slots,) + unit, BF),
         pltpu.VMEM((slots,) + unit, BF),
-        pltpu.VMEM((LATE,) + unit, BF),
-        pltpu.VMEM((LATE,) + unit, BF),
+        pltpu.VMEM((EARLY,) + unit, BF),
         pltpu.VMEM((slots,) + unit, BF),
         pltpu.VMEM((slots,) + unit, BF),
-        pltpu.VMEM((LATE,) + unit, BF),
         pltpu.VMEM((slots,) + unit, BF),
         pltpu.VMEM(unit, F32),
         pltpu.VMEM(unit, F32),
@@ -656,20 +664,20 @@
         dma,
         dma((2,)),
         dma((2,)),
-        dma((rows_n,)),
-        dma((rows_n,)),
-        dma((rows_n,)),
-        dma((rows_n,)),
+        dma,
+        dma,
+        dma,
+        dma,
         dma((2,)),
         dma((2,)),
         dma((slots,)),
+        dma,
         dma((slots,)),
-        dma((slots,)),
-        dma((slots,)),
-        dma((dp_n,)),
-        dma((dp_n,)),
-        dma((rows_n,)),
-        dma((rows_n,)),
+        dma,
+        dma,
+        dma,
+        dma,
+        dma,
     ]
 
     def body(*refs):

time: 55.3 us -> 51.6 us (0.933)
  Pallas kernels: 54.5 us -> 50.8 us
    pallas_call x1, Pallas kernels: 53.7 us -> 50 us  [shards(): pl.pallas_call(body, out_shape=(jax.ShapeDtypeStruct((1, 1, half, OUTS),...]
where the time goes in v4:
time: 51.6 us; the launch traced here: 51.4 us
  Pallas kernels  50.8 us (98%)
  between operations  0.64 us (1%)
    pallas_call x1, Pallas kernels, shards(): pl.pallas_call(body, out_shape=(jax.ShapeDtypeStruct((1, 1, half, OUTS),...  50 us

profile of v4, /device:TPU:1, one launch (start us, length us, event | category | flops | bytes accessed | tf_op | source)
XLA Modules:
  0.0 51.4 jit_solution(1062658543238378659)
XLA Ops:
  0.6 50.0 %step.1 = (bf16[1,1,256,256]{3,2,1,0:T(8,128)(2,1)S(1)}, bf16[1,2,512,128]{3,2,1,0:T(8,128)(2,1)S(1)}, f32[16,8,128]{2,1,0:T(8,128)S(1)}) custom-call(bf16[1,2,512,128]{3,2,1,0:T(8,128)(2,1)} %refs_0_.1, bf16[3,3,128,128]{3,2,1,0:T(8,128)(2,1)} %refs_1_.1, f32[1,128]{1,0:T(1,128)} %bitcast.17, f32[1,128]{1,0:T(1,128)} %bitcast.18, f32[1,128]{1,0:T(1,128)} %bitcast.19, ...), custom_call_target="tpu_custom_call" | custom-call | tf_op jit(solution)/shard_map/step/pallas_call | solution.py:686
  50.6 0.8 %finish.1 = (bf16[1,1,256,256]{3,2,1,0:T(8,128)(2,1)}, bf16[1,2,512,128]{3,2,1,0:T(8,128)(2,1)}, f32[9,4,128]{2,1,0:T(4,128)}, f32[1,4]{1,0:T(1,128)}, f32[1,4]{...) custom-call(bf16[1,1,256,256]{3,2,1,0:T(8,128)(2,1)S(1)} %get-tuple-element.19.block, ...), custom_call_target="tpu_custom_call" | custom-call | tf_op jit(solution)/shard_map/finish/pallas_call | solution.py:711

commit v5 on v4

--- a/solution.py
+++ b/solution.py
@@ -14,6 +14,7 @@
 EPS = 1e-05
 TAPS = 9
 EARLY = 6
+FIRST = 5
 
 
 def nn(a, b):
@@ -117,6 +118,8 @@
     d_r,
     o_s,
     o_r,
+    mates_in,
+    dp_in,
 ):
     r = lax.axis_index("rows")
     d = lax.axis_index("dp")
@@ -179,17 +182,37 @@
         dp_peers = [lax.rem(d + i, dp_n) for i in range(1, dp_n)]
 
     barrier = pltpu.get_barrier_semaphore()
-    for to in dp_peers:
-        pl.semaphore_signal(barrier, inc=1, device_id={"dp": to}, device_id_type=MESH)
-    for to in row_peers:
-        pl.semaphore_signal(barrier, inc=1, device_id={"rows": to}, device_id_type=MESH)
+    slot_peers = [
+        lax.rem(x_at + dx, 4) * 2 + (y_at if dy == 0 else 1 - y_at)
+        for dx, dy in ((2, 1), (2, 0), (1, 1), (3, 1), (1, 0), (3, 0), (0, 1))
+    ]
+    if dp_n == 32:
+        z_peers = [lax.rem(z_at + dz, 8) * 4 + h_at for dz in (4, 3, 5, 2, 6, 1, 7)]
+        h_peers = [z_at * 4 + lax.rem(h_at + dh, 4) for dh in (2, 1, 3)]
+    else:
+        z_peers, h_peers = dp_peers, []
+    up = lax.max(r - 1, 0)
+    down = lax.min(r + 1, last)
+
+    def greet(sem, **where):
+        pl.semaphore_signal(sem, inc=1, device_id=where, device_id_type=MESH)
+
+    for to in z_peers + h_peers:
+        greet(barrier, dp=to)
+    for to in slot_peers:
+        greet(barrier, rows=2 * to + core)
+    greet(barrier, rows=mate)
+    far = r - 1 + 2 * core
+    far_is = (far >= 0) & (far <= last)
+
+    @pl.when(far_is)
+    def _():
+        greet(barrier, rows=lax.min(lax.max(far, 0), last))
 
     for load in loads:
         load.start()
 
-    pl.semaphore_wait(barrier, rows_n + dp_n - 2)
-    up = lax.max(r - 1, 0)
-    down = lax.min(r + 1, last)
+    pl.semaphore_wait(barrier, slots + len(z_peers) + len(h_peers) + jnp.where(far_is, 1, 0))
     mid = pl.ds(CHANS, 2 * CHANS)
     img_down = remote(img_hbm.at[0, 1], edge_img.at[0], img_s.at[0], img_r.at[0], rows=down)
     img_up = remote(img_hbm.at[0, 0], edge_img.at[1], img_s.at[1], img_r.at[1], rows=up)
@@ -206,6 +229,12 @@
     def _():
         img_up.start()
         cot_up.start()
+
+    for to in slot_peers:
+        greet(mates_in, rows=2 * to + core)
+    if h_peers:
+        for to in z_peers:
+            greet(dp_in, dp=to)
 
     loads[1].wait()
     zero_block = jnp.zeros((CHANS, CHANS), BF)
@@ -290,6 +319,7 @@
     stat_a[r, 0:1, :] = own_sum
     stat_a[r, 1:2, :] = own_sq
     stat_a[r, 2:8, :] = jnp.zeros((6, CHANS), F32)
+    pl.semaphore_wait(mates_in, slots - 1)
     spread(stat_a, sa_s, sa_r)
 
     @pl.when(r < last)
@@ -367,8 +397,8 @@
                 early[0, tap - 3] = low
                 early[1, tap - 3] = high
             else:
-                late[1, 4 + tap] = low
-                late[0, 5 + tap] = high
+                late[0, 4 + tap] = low
+                late[1, 5 + tap] = high
 
     def taps(kh):
         return dw[kh].reshape(3 * CHANS, OUTS)
@@ -380,21 +410,30 @@
     down_grad(2)
     cs[...] = early[1 - core].astype(BF)
     pair_one = remote(cs, cr, c_s.at[0], c_r.at[0], rows=mate)
-    pair_two = remote(cs2, cr2, c_s.at[1], c_r.at[1], rows=mate)
+    pair_two = remote(cs2.at[0:FIRST], cr2.at[0:FIRST], c_s.at[1], c_r.at[1], rows=mate)
+    pair_rest = remote(cs2.at[FIRST:], cr2.at[FIRST:], c_s.at[2], c_r.at[2], rows=mate)
     pair_one.start()
     out = nn(m4[1], taps(1)) + nn(m4[2], taps(2)) + db[...]
     hold[...] = out
 
-    slot_peers = [
-        lax.rem(x_at + dx, 4) * 2 + (y_at if dy == 0 else 1 - y_at)
-        for dx, dy in ((2, 1), (2, 0), (1, 1), (3, 1), (1, 0), (3, 0), (0, 1))
-    ]
-
     def early_send(to):
         return remote(rs.at[lax.min(to, EARLY - 1)], rr.at[slot], r_s.at[to], r_r, rows=2 * to + core)
 
     def late_send(to):
-        return remote(rs2.at[to], rr2.at[slot], q_s.at[to], q_r, rows=2 * to + core)
+        return remote(rs2.at[number(to)], rr2.at[slot], q_s.at[to], q_r, rows=2 * to + core)
+
+    def number(at):
+        return lax.div(at, 2) + 4 * lax.rem(at + core, 2)
+
+    def late_sum(low, high):
+        both = late[core, low:high] + cr2[low:high].astype(F32)
+        late[core, low:high] = both
+        rs2[low:high] = both.astype(BF)
+        for to in slot_peers:
+
+            @pl.when((number(to) >= low) & (number(to) < high))
+            def _():
+                late_send(to).start()
 
     pair_one.wait()
     both = early[core] + cr[...].astype(F32)
@@ -412,7 +451,13 @@
         m4[0, :, :CHANS] = shifted(m4[0, :, 2 * CHANS :].astype(F32), -1).astype(BF)
 
     down_grad(0)
+    late[0, 7] = jnp.zeros((CHANS, CHANS), F32)
+    cs2[FIRST:] = late[1 - core, FIRST:].astype(BF)
+    pair_rest.start()
     block_out[0, 0] = (hold[...] + nn(m4[0], taps(0))).astype(BF)
+
+    pair_rest.wait()
+    late_sum(FIRST, slots)
 
     whole(stat_b, sb_s, sb_r).wait_recv()
     totals = jnp.sum(stat_b[...], axis=0)
@@ -444,12 +489,11 @@
         )
         for kw in range(3):
             tap = 3 * kh + kw
-            late[tap % 2, tap // 2] = (
+            late[tap % 2 if tap < 8 else 1, tap // 2] = (
                 part[:CHANS, kw * CHANS : (kw + 1) * CHANS]
                 + part[CHANS:, (kw + 1) * CHANS : (kw + 2) * CHANS]
             )
-    late[1, 7] = jnp.zeros((CHANS, CHANS), F32)
-    cs2[...] = late[1 - core].astype(BF)
+    cs2[:FIRST] = late[1 - core, :FIRST].astype(BF)
     pair_two.start()
 
     def sides(f):
@@ -458,11 +502,7 @@
         g4[f, :, 3 * CHANS :] = shifted(grad[:, :CHANS], 1).astype(BF)
 
     pair_two.wait()
-    both = late[core] + cr2[...].astype(F32)
-    late[core] = both
-    rs2[...] = both.astype(BF)
-    for to in slot_peers:
-        late_send(to).start()
+    late_sum(0, FIRST)
 
     @pl.when(r < last)
     def _():
@@ -492,7 +532,7 @@
         red1[...] = jnp.broadcast_to(mine[core][None], (16, 8, CHANS)).reshape(CHANS, CHANS)
 
     remote(rr2.at[others], rr2.at[others], q_s.at[slot], q_r, rows=mate).wait_recv()
-    total = late[core, slot]
+    total = late[core, number(slot)]
     for other in slot_peers:
         total = total + rr2[other].astype(F32)
     red2[...] = total
@@ -505,6 +545,8 @@
         row = lax.rem(e, 2) * 16 + lax.div(e, 2)
         return pl.ds(pl.multiple_of(row * 8, 8), 8)
 
+    if h_peers:
+        pl.semaphore_wait(dp_in, len(z_peers))
     for to in dp_peers:
         remote(red.at[place(to)], dr.at[d], d_s, d_r, dp=to).start()
     dr[d] = red[place(d), :]
@@ -584,10 +626,10 @@
     copies[0].start()
     copies[1].start()
     for tap in range(TAPS):
-        conv_v[tap] = table[tap, 4:8]
+        conv_v[tap] = table[2 * tap + tap % 2 if tap < 8 else 1, 4:8]
         if tap < 3:
-            down_v[tap, 0:4] = table[9 + 2 * tap, 4:8]
-            down_v[tap, 4:8] = table[10 + 2 * tap, 4:8]
+            down_v[tap, 0:4] = table[2 + 4 * tap, 4:8]
+            down_v[tap, 4:8] = table[5 + 4 * tap, 4:8]
         else:
             down_v[tap, 0:4] = table[2 * tap - 6, 0:4]
             down_v[tap, 4:8] = table[2 * tap - 5, 0:4]
@@ -668,8 +710,8 @@
         dma,
         dma,
         dma,
-        dma((2,)),
-        dma((2,)),
+        dma((3,)),
+        dma((3,)),
         dma((slots,)),
         dma,
         dma((slots,)),
@@ -678,6 +720,8 @@
         dma,
         dma,
         dma,
+        pltpu.SemaphoreType.REGULAR,
+        pltpu.SemaphoreType.REGULAR,
     ]
 
     def body(*refs):

time: 51.6 us -> 50.2 us (0.973)
  Pallas kernels: 50.8 us -> 49.5 us
    pallas_call x1, Pallas kernels: 50 us -> 48.6 us  [shards(): pl.pallas_call(body, out_shape=(jax.ShapeDtypeStruct((1, 1, half, OUTS),...]
where the time goes in v5:
time: 50.2 us; the launch traced here: 50.1 us
  Pallas kernels  49.5 us (99%)
  between operations  0.64 us (1%)
    pallas_call x1, Pallas kernels, shards(): pl.pallas_call(body, out_shape=(jax.ShapeDtypeStruct((1, 1, half, OUTS),...  48.6 us

profile of v5, /device:TPU:1, one launch (start us, length us, event | category | flops | bytes accessed | tf_op | source)
XLA Modules:
  0.0 50.1 jit_solution(10121937647995243776)
XLA Ops:
  0.6 48.6 %step.1 = (bf16[1,1,256,256]{3,2,1,0:T(8,128)(2,1)S(1)}, bf16[1,2,512,128]{3,2,1,0:T(8,128)(2,1)S(1)}, f32[16,8,128]{2,1,0:T(8,128)S(1)}) custom-call(bf16[1,2,512,128]{3,2,1,0:T(8,128)(2,1)} %refs_0_.1, bf16[3,3,128,128]{3,2,1,0:T(8,128)(2,1)} %refs_1_.1, f32[1,128]{1,0:T(1,128)} %bitcast.17, f32[1,128]{1,0:T(1,128)} %bitcast.18, f32[1,128]{1,0:T(1,128)} %bitcast.19, ...), custom_call_target="tpu_custom_call" | custom-call | tf_op jit(solution)/shard_map/step/pallas_call | solution.py:730
  49.3 0.8 %finish.1 = (bf16[1,1,256,256]{3,2,1,0:T(8,128)(2,1)}, bf16[1,2,512,128]{3,2,1,0:T(8,128)(2,1)}, f32[9,4,128]{2,1,0:T(4,128)}, f32[1,4]{1,0:T(1,128)}, f32[1,4]{...) custom-call(bf16[1,1,256,256]{3,2,1,0:T(8,128)(2,1)S(1)} %get-tuple-element.19.block, ...), custom_call_target="tpu_custom_call" | custom-call | tf_op jit(solution)/shard_map/finish/pallas_call | solution.py:755

commit v6 on v5

--- a/solution.py
+++ b/solution.py
@@ -118,8 +118,7 @@
     d_r,
     o_s,
     o_r,
-    mates_in,
-    dp_in,
+    met,
 ):
     r = lax.axis_index("rows")
     d = lax.axis_index("dp")
@@ -188,19 +187,21 @@
     ]
     if dp_n == 32:
         z_peers = [lax.rem(z_at + dz, 8) * 4 + h_at for dz in (4, 3, 5, 2, 6, 1, 7)]
-        h_peers = [z_at * 4 + lax.rem(h_at + dh, 4) for dh in (2, 1, 3)]
+        dp_near = z_peers[-2:] + [z_at * 4 + lax.rem(h_at + dh, 4) for dh in (1, 3)]
     else:
-        z_peers, h_peers = dp_peers, []
+        z_peers, dp_near = [], dp_peers
+    x_peers = [lax.rem(r + 4 * dx, rows_n) for dx in (2, 1, 3)]
+    y_peer = r + 2 - 4 * y_at
     up = lax.max(r - 1, 0)
     down = lax.min(r + 1, last)
 
     def greet(sem, **where):
         pl.semaphore_signal(sem, inc=1, device_id=where, device_id_type=MESH)
 
-    for to in z_peers + h_peers:
+    for to in dp_near:
         greet(barrier, dp=to)
-    for to in slot_peers:
-        greet(barrier, rows=2 * to + core)
+    for to in x_peers[1:] + [y_peer]:
+        greet(barrier, rows=to)
     greet(barrier, rows=mate)
     far = r - 1 + 2 * core
     far_is = (far >= 0) & (far <= last)
@@ -212,7 +213,7 @@
     for load in loads:
         load.start()
 
-    pl.semaphore_wait(barrier, slots + len(z_peers) + len(h_peers) + jnp.where(far_is, 1, 0))
+    pl.semaphore_wait(barrier, 4 + len(dp_near) + jnp.where(far_is, 1, 0))
     mid = pl.ds(CHANS, 2 * CHANS)
     img_down = remote(img_hbm.at[0, 1], edge_img.at[0], img_s.at[0], img_r.at[0], rows=down)
     img_up = remote(img_hbm.at[0, 0], edge_img.at[1], img_s.at[1], img_r.at[1], rows=up)
@@ -230,11 +231,11 @@
         img_up.start()
         cot_up.start()
 
-    for to in slot_peers:
-        greet(mates_in, rows=2 * to + core)
-    if h_peers:
-        for to in z_peers:
-            greet(dp_in, dp=to)
+    for to in x_peers[1:] + [y_peer]:
+        greet(met.at[0], rows=to)
+    if z_peers:
+        for to in dp_near:
+            greet(met.at[1], dp=to)
 
     loads[1].wait()
     zero_block = jnp.zeros((CHANS, CHANS), BF)
@@ -286,6 +287,14 @@
     hid[0] = nn(x4[1], wf[1]) + nn(x4[2], wf[2]) + bias
     hid[1] = nn(x4[1], wf[0]) + nn(x4[2], wf[1]) + bias
 
+    pl.semaphore_wait(met.at[0], 3)
+    for to in x_peers:
+        greet(met.at[2], rows=to)
+    if z_peers:
+        pl.semaphore_wait(met.at[1], len(dp_near))
+        for to in z_peers[3:5]:
+            greet(met.at[3], dp=to)
+
     @pl.when(r > 0)
     def _():
         img_down.wait_recv()
@@ -319,8 +328,12 @@
     stat_a[r, 0:1, :] = own_sum
     stat_a[r, 1:2, :] = own_sq
     stat_a[r, 2:8, :] = jnp.zeros((6, CHANS), F32)
-    pl.semaphore_wait(mates_in, slots - 1)
+    pl.semaphore_wait(met.at[2], 3)
     spread(stat_a, sa_s, sa_r)
+    if z_peers:
+        pl.semaphore_wait(met.at[3], 2)
+        for to in z_peers:
+            greet(met.at[4], dp=to)
 
     @pl.when(r < last)
     def _():
@@ -545,8 +558,8 @@
         row = lax.rem(e, 2) * 16 + lax.div(e, 2)
         return pl.ds(pl.multiple_of(row * 8, 8), 8)
 
-    if h_peers:
-        pl.semaphore_wait(dp_in, len(z_peers))
+    if z_peers:
+        pl.semaphore_wait(met.at[4], len(z_peers))
     for to in dp_peers:
         remote(red.at[place(to)], dr.at[d], d_s, d_r, dp=to).start()
     dr[d] = red[place(d), :]
@@ -720,8 +733,7 @@
         dma,
         dma,
         dma,
-        pltpu.SemaphoreType.REGULAR,
-        pltpu.SemaphoreType.REGULAR,
+        pltpu.SemaphoreType.REGULAR((5,)),
     ]
 
     def body(*refs):

time: 50.2 us -> 50.2 us (level)
  no operation moved by 1% of the time
where the time goes in v6:
time: 50.2 us; the launch traced here: 50.1 us
  Pallas kernels  49.4 us (98%)
  between operations  0.64 us (1%)
    pallas_call x1, Pallas kernels, shards(): pl.pallas_call(body, out_shape=(jax.ShapeDtypeStruct((1, 1, half, OUTS),...  48.6 us

profile of v6, /device:TPU:1, one launch (start us, length us, event | category | flops | bytes accessed | tf_op | source)
XLA Modules:
  0.0 50.1 jit_solution(9685230913689182458)
XLA Ops:
  0.6 48.6 %step.1 = (bf16[1,1,256,256]{3,2,1,0:T(8,128)(2,1)S(1)}, bf16[1,2,512,128]{3,2,1,0:T(8,128)(2,1)S(1)}, f32[16,8,128]{2,1,0:T(8,128)S(1)}) custom-call(bf16[1,2,512,128]{3,2,1,0:T(8,128)(2,1)} %refs_0_.1, bf16[3,3,128,128]{3,2,1,0:T(8,128)(2,1)} %refs_1_.1, f32[1,128]{1,0:T(1,128)} %bitcast.17, f32[1,128]{1,0:T(1,128)} %bitcast.18, f32[1,128]{1,0:T(1,128)} %bitcast.19, ...), custom_call_target="tpu_custom_call" | custom-call | tf_op jit(solution)/shard_map/step/pallas_call | solution.py:742
  49.2 0.8 %finish.1 = (bf16[1,1,256,256]{3,2,1,0:T(8,128)(2,1)}, bf16[1,2,512,128]{3,2,1,0:T(8,128)(2,1)}, f32[9,4,128]{2,1,0:T(4,128)}, f32[1,4]{1,0:T(1,128)}, f32[1,4]{...) custom-call(bf16[1,1,256,256]{3,2,1,0:T(8,128)(2,1)S(1)} %get-tuple-element.19.block, ...), custom_call_target="tpu_custom_call" | custom-call | tf_op jit(solution)/shard_map/finish/pallas_call | solution.py:767

commit v7 on v6

--- a/solution.py
+++ b/solution.py
@@ -295,19 +295,21 @@
         for to in z_peers[3:5]:
             greet(met.at[3], dp=to)
 
-    @pl.when(r > 0)
-    def _():
-        img_down.wait_recv()
-
-    split_columns(edge_img[0], 0)
-    hid[0] += nn(x4[0], wf[0])
-
-    @pl.when(r < last)
-    def _():
-        img_up.wait_recv()
-
-    split_columns(edge_img[1], 3)
-    hid[1] += nn(x4[3], wf[2])
+    def add_edge(e):
+        split_columns(edge_img[e], 3 * e)
+        hid[e] += nn(x4[3 * e], wf[2 * e])
+
+    def edge_in(e):
+        remote(img_hbm.at[0, 0], edge_img.at[e], img_s.at[0], img_r.at[e], rows=mate).wait_recv()
+
+    edge_in(1 - core)
+    add_edge(1 - core)
+
+    @pl.when(far_is)
+    def _():
+        edge_in(core)
+
+    add_edge(core)
 
     def spread(table, send, recv):
         for to in row_peers:

time: 50.2 us -> 49.9 us (level)
  no operation moved by 1% of the time
where the time goes in v7:
time: 49.9 us; the launch traced here: 49.8 us
  Pallas kernels  49.1 us (98%)
  between operations  0.64 us (1%)
    pallas_call x1, Pallas kernels, shards(): pl.pallas_call(body, out_shape=(jax.ShapeDtypeStruct((1, 1, half, OUTS),...  48.3 us

profile of v7, /device:TPU:1, one launch (start us, length us, event | category | flops | bytes accessed | tf_op | source)
XLA Modules:
  0.0 49.8 jit_solution(3948823515798026382)
XLA Ops:
  0.6 48.3 %step.1 = (bf16[1,1,256,256]{3,2,1,0:T(8,128)(2,1)S(1)}, bf16[1,2,512,128]{3,2,1,0:T(8,128)(2,1)S(1)}, f32[16,8,128]{2,1,0:T(8,128)S(1)}) custom-call(bf16[1,2,512,128]{3,2,1,0:T(8,128)(2,1)} %refs_0_.1, bf16[3,3,128,128]{3,2,1,0:T(8,128)(2,1)} %refs_1_.1, f32[1,128]{1,0:T(1,128)} %bitcast.17, f32[1,128]{1,0:T(1,128)} %bitcast.18, f32[1,128]{1,0:T(1,128)} %bitcast.19, ...), custom_call_target="tpu_custom_call" | custom-call | tf_op jit(solution)/shard_map/step/pallas_call | solution.py:744
  48.9 0.8 %finish.1 = (bf16[1,1,256,256]{3,2,1,0:T(8,128)(2,1)}, bf16[1,2,512,128]{3,2,1,0:T(8,128)(2,1)}, f32[9,4,128]{2,1,0:T(4,128)}, f32[1,4]{1,0:T(1,128)}, f32[1,4]{...) custom-call(bf16[1,1,256,256]{3,2,1,0:T(8,128)(2,1)S(1)} %get-tuple-element.19.block, ...), custom_call_target="tpu_custom_call" | custom-call | tf_op jit(solution)/shard_map/finish/pallas_call | solution.py:769

commit v8 on v7

--- a/solution.py
+++ b/solution.py
@@ -469,10 +469,6 @@
     late[0, 7] = jnp.zeros((CHANS, CHANS), F32)
     cs2[FIRST:] = late[1 - core, FIRST:].astype(BF)
     pair_rest.start()
-    block_out[0, 0] = (hold[...] + nn(m4[0], taps(0))).astype(BF)
-
-    pair_rest.wait()
-    late_sum(FIRST, slots)
 
     whole(stat_b, sb_s, sb_r).wait_recv()
     totals = jnp.sum(stat_b[...], axis=0)
@@ -516,6 +512,9 @@
         g4[f, :, :CHANS] = shifted(grad[:, CHANS:], -1).astype(BF)
         g4[f, :, 3 * CHANS :] = shifted(grad[:, :CHANS], 1).astype(BF)
 
+    pair_rest.wait()
+    late_sum(FIRST, slots)
+
     pair_two.wait()
     late_sum(0, FIRST)
 
@@ -527,6 +526,7 @@
     def _():
         g_up.start()
 
+    block_out[0, 0] = (hold[...] + nn(m4[0], taps(0))).astype(BF)
     sides(1)
     sides(2)
     gmix[0] += nt(g4[1], wb[1]) + nt(g4[2], wb[0])

time: 49.9 us -> 49.6 us (level)
  no operation moved by 1% of the time
where the time goes in v8:
time: 49.6 us; the launch traced here: 49.5 us
  Pallas kernels  48.9 us (99%)
  between operations  0.64 us (1%)
    pallas_call x1, Pallas kernels, shards(): pl.pallas_call(body, out_shape=(jax.ShapeDtypeStruct((1, 1, half, OUTS),...  48 us

profile of v8, /device:TPU:1, one launch (start us, length us, event | category | flops | bytes accessed | tf_op | source)
XLA Modules:
  0.0 49.5 jit_solution(18244427428866532404)
XLA Ops:
  0.6 48.0 %step.1 = (bf16[1,1,256,256]{3,2,1,0:T(8,128)(2,1)S(1)}, bf16[1,2,512,128]{3,2,1,0:T(8,128)(2,1)S(1)}, f32[16,8,128]{2,1,0:T(8,128)S(1)}) custom-call(bf16[1,2,512,128]{3,2,1,0:T(8,128)(2,1)} %refs_0_.1, bf16[3,3,128,128]{3,2,1,0:T(8,128)(2,1)} %refs_1_.1, f32[1,128]{1,0:T(1,128)} %bitcast.17, f32[1,128]{1,0:T(1,128)} %bitcast.18, f32[1,128]{1,0:T(1,128)} %bitcast.19, ...), custom_call_target="tpu_custom_call" | custom-call | tf_op jit(solution)/shard_map/step/pallas_call | solution.py:744
  48.7 0.8 %finish.1 = (bf16[1,1,256,256]{3,2,1,0:T(8,128)(2,1)}, bf16[1,2,512,128]{3,2,1,0:T(8,128)(2,1)}, f32[9,4,128]{2,1,0:T(4,128)}, f32[1,4]{1,0:T(1,128)}, f32[1,4]{...) custom-call(bf16[1,1,256,256]{3,2,1,0:T(8,128)(2,1)S(1)} %get-tuple-element.19.block, ...), custom_call_target="tpu_custom_call" | custom-call | tf_op jit(solution)/shard_map/finish/pallas_call | solution.py:769
